TPU v7x, 32 devices: a whole 2x2x4 slice. The times are simulated.
32 devices in a mesh: fsdp: 16 (over z, y, core), ctx: 2 (over x).
Axes of the slice: x: 2, y: 2, z: 4, core: 2. Of those that a mesh axis runs over, the one named last changes fastest.
Arguments:
- tokens: bfloat16 [16, 512, 384], P('fsdp', 'ctx'), may hold values from -6 to 6
- condition: bfloat16 [16, 384], P('fsdp'), may hold values from -6 to 6
- ada_weight: bfloat16 [384, 2304], P('fsdp'), may hold values from -0.3125 to 0.3125
- ada_bias: bfloat16 [2304], P('fsdp'), may hold values from -5 to 5
- qkv_weight: bfloat16 [384, 1152], P('fsdp'), may hold values from -1 to 1
- qv_bias: bfloat16 [768], P('fsdp'), may hold values from -5 to 5
- out_weight: bfloat16 [384, 384], P('fsdp'), may hold values from -2.5 to 2.5
- out_bias: bfloat16 [384], P('fsdp'), may hold values from -5 to 5
- fc1_weight: bfloat16 [384, 1536], P('fsdp'), may hold values from -0.3125 to 0.3125
- fc1_bias: bfloat16 [1536], P('fsdp'), may hold values from -5 to 5
- fc2_weight: bfloat16 [1536, 384], P('fsdp'), may hold values from -0.15625 to 0.15625
- fc2_bias: bfloat16 [384], P('fsdp'), may hold values from -5 to 5
- cotangent: bfloat16 [16, 512, 384], P('fsdp', 'ctx'), may hold values from -6 to 6
Outputs:
- output: bfloat16 [16, 512, 384], P('fsdp', 'ctx')
- grad_tokens: bfloat16 [16, 512, 384], P('fsdp', 'ctx')
- grad_condition: float32 [16, 384], P('fsdp')
- grad_ada_weight: float32 [384, 2304], P('fsdp')
- grad_ada_bias: float32 [2304], P('fsdp')
- grad_qkv_weight: float32 [384, 1152], P('fsdp')
- grad_qv_bias: float32 [768], P('fsdp')
- grad_out_weight: float32 [384, 384], P('fsdp')
- grad_out_bias: float32 [384], P('fsdp')
- grad_fc1_weight: float32 [384, 1536], P('fsdp')
- grad_fc1_bias: float32 [1536], P('fsdp')
- grad_fc2_weight: float32 [1536, 384], P('fsdp')
- grad_fc2_bias: float32 [384], P('fsdp')
All inputs are finite; a program needn't handle non-finite values.
Results may differ from a plain program's by a relative error of at most 0.022.
Values may be sent and summed in bfloat16 or wider, within the bound.
A program may use at most 64 MiB of HBM per device.

v0:
```python
from functools import partial

import jax
import jax.numpy as jnp
from jax import lax
from jax.sharding import PartitionSpec as P

HEADS = 6
HEAD = 64


epsilon = 1e-06


def layer_stats(values):
    centered = values - jnp.mean(values, axis=-1, keepdims=True)
    inverse = lax.rsqrt(jnp.mean(centered * centered, axis=-1, keepdims=True) + epsilon)
    return (centered * inverse, inverse)


def layer_back(normed, inverse, grad_normed):
    mean_grad = jnp.mean(grad_normed, axis=-1, keepdims=True)
    mean_prod = jnp.mean(grad_normed * normed, axis=-1, keepdims=True)
    return inverse * (grad_normed - mean_grad - normed * mean_prod)


def gelu_back(hidden, grad_output):
    return jax.vjp(partial(jax.nn.gelu, approximate=True), hidden)[1](grad_output)[0]


def per_device(
    tokens,
    condition,
    ada_weight,
    ada_bias,
    qkv_weight,
    qv_bias,
    out_weight,
    out_bias,
    fc1_weight,
    fc1_bias,
    fc2_weight,
    fc2_bias,
    cotangent,
):
    latents, local_rows, model_width = tokens.shape
    scale_factor = HEAD ** (-0.5)
    (
        ada_full,
        ada_bias_full,
        qkv_full,
        qv_bias_full,
        out_full,
        out_bias_full,
        fc1_full,
        fc1_bias_full,
        fc2_full,
        fc2_bias_full,
    ) = (
        lax.all_gather(ada_weight, "fsdp", axis=0, tiled=True),
        lax.all_gather(ada_bias, "fsdp", axis=0, tiled=True),
        lax.all_gather(qkv_weight, "fsdp", axis=0, tiled=True),
        lax.all_gather(qv_bias, "fsdp", axis=0, tiled=True),
        lax.all_gather(out_weight, "fsdp", axis=0, tiled=True),
        lax.all_gather(out_bias, "fsdp", axis=0, tiled=True),
        lax.all_gather(fc1_weight, "fsdp", axis=0, tiled=True),
        lax.all_gather(fc1_bias, "fsdp", axis=0, tiled=True),
        lax.all_gather(fc2_weight, "fsdp", axis=0, tiled=True),
        lax.all_gather(fc2_bias, "fsdp", axis=0, tiled=True),
    )
    cond_float = condition.astype(jnp.float32)
    cond_silu = jax.nn.silu(cond_float).astype(jnp.bfloat16)
    modulation = jnp.dot(
        cond_silu, ada_full, preferred_element_type=jnp.float32
    ) + ada_bias_full.astype(jnp.float32)
    shift_one, scale_one, gate_one, shift_two, scale_two, gate_two = jnp.split(
        modulation[:, None, :], 6, axis=2
    )
    residual = tokens.astype(jnp.float32)
    normed_one, inverse_one = layer_stats(residual)
    hidden_one = (normed_one * (1.0 + scale_one) + shift_one).astype(jnp.bfloat16)
    projected = jnp.einsum("bsd,de->bse", hidden_one, qkv_full, preferred_element_type=jnp.float32)
    bias_float = qv_bias_full.astype(jnp.float32)
    queries = (projected[..., :model_width] + bias_float[:model_width]).astype(jnp.bfloat16)
    keys = projected[..., model_width : 2 * model_width].astype(jnp.bfloat16)
    values = (projected[..., 2 * model_width :] + bias_float[model_width:]).astype(jnp.bfloat16)
    query_four = queries.reshape(latents, local_rows, HEADS, HEAD)
    whole_keys, whole_values = (
        lax.all_gather(keys, "ctx", axis=1, tiled=True),
        lax.all_gather(values, "ctx", axis=1, tiled=True),
    )
    blocks = whole_keys.shape[1] // local_rows
    key_blocks = jnp.moveaxis(whole_keys.reshape(latents, blocks, local_rows, HEADS, HEAD), 1, 0)
    value_blocks = jnp.moveaxis(
        whole_values.reshape(latents, blocks, local_rows, HEADS, HEAD), 1, 0
    )

    def statistic_step(state, key_block):
        running_max, running_sum = state
        scores = (
            jnp.einsum("bqhd,bkhd->bhqk", query_four, key_block, preferred_element_type=jnp.float32)
            * scale_factor
        )
        new_max = jnp.maximum(running_max, jnp.max(scores, axis=3))
        running_sum = running_sum * jnp.exp(running_max - new_max) + jnp.sum(
            jnp.exp(scores - new_max[..., None]), axis=3
        )
        return ((new_max, running_sum), None)

    stat_start = (
        jnp.full((latents, HEADS, local_rows), -1e30, jnp.float32),
        jnp.zeros((latents, HEADS, local_rows), jnp.float32),
    )
    (final_max, final_sum), unused = lax.scan(statistic_step, stat_start, key_blocks)
    log_total = final_max + jnp.log(final_sum)

    def mixing_step(accumulated, pair_items):
        key_block, value_block = pair_items
        scores = (
            jnp.einsum("bqhd,bkhd->bhqk", query_four, key_block, preferred_element_type=jnp.float32)
            * scale_factor
        )
        weights = jnp.exp(scores - log_total[..., None]).astype(jnp.bfloat16)
        return (
            accumulated
            + jnp.einsum(
                "bhqk,bkhd->bhqd", weights, value_block, preferred_element_type=jnp.float32
            ),
            None,
        )

    final_acc, unused = lax.scan(
        mixing_step,
        jnp.zeros((latents, HEADS, local_rows, HEAD), jnp.float32),
        (key_blocks, value_blocks),
    )
    mixed = (
        final_acc.transpose(0, 2, 1, 3)
        .reshape(latents, local_rows, model_width)
        .astype(jnp.bfloat16)
    )
    attn_out = jnp.einsum(
        "bsd,de->bse", mixed, out_full, preferred_element_type=jnp.float32
    ) + out_bias_full.astype(jnp.float32)
    after_attn = residual + gate_one * attn_out
    normed_two, inverse_two = layer_stats(after_attn)
    hidden_two = (normed_two * (1.0 + scale_two) + shift_two).astype(jnp.bfloat16)
    pre_act = jnp.einsum(
        "bsd,df->bsf", hidden_two, fc1_full, preferred_element_type=jnp.float32
    ) + fc1_bias_full.astype(jnp.float32)
    activated = jax.nn.gelu(pre_act, approximate=True).astype(jnp.bfloat16)
    mlp_out = jnp.einsum(
        "bsf,fd->bsd", activated, fc2_full, preferred_element_type=jnp.float32
    ) + fc2_bias_full.astype(jnp.float32)
    result = (after_attn + gate_two * mlp_out).astype(jnp.bfloat16)
    ada_back, qkv_back, out_back, fc1_back, fc2_back = (
        lax.all_gather(ada_weight, "fsdp", axis=0, tiled=True),
        lax.all_gather(qkv_weight, "fsdp", axis=0, tiled=True),
        lax.all_gather(out_weight, "fsdp", axis=0, tiled=True),
        lax.all_gather(fc1_weight, "fsdp", axis=0, tiled=True),
        lax.all_gather(fc2_weight, "fsdp", axis=0, tiled=True),
    )
    grad_result = cotangent.astype(jnp.float32)
    grad_gate_two = jnp.sum(grad_result * mlp_out, axis=1)
    grad_mlp_float = grad_result * gate_two
    grad_mlp = grad_mlp_float.astype(jnp.bfloat16)
    grad_fc2_w = jnp.einsum("bsf,bsd->fd", activated, grad_mlp, preferred_element_type=jnp.float32)
    grad_fc2_b = jnp.sum(grad_mlp_float, axis=(0, 1))
    grad_act = jnp.einsum("bsd,fd->bsf", grad_mlp, fc2_back, preferred_element_type=jnp.float32)
    grad_pre = gelu_back(pre_act, grad_act)
    grad_pre_half = grad_pre.astype(jnp.bfloat16)
    grad_fc1_w = jnp.einsum(
        "bsd,bsf->df", hidden_two, grad_pre_half, preferred_element_type=jnp.float32
    )
    grad_fc1_b = jnp.sum(grad_pre, axis=(0, 1))
    grad_hidden_two = jnp.einsum(
        "bsf,df->bsd", grad_pre_half, fc1_back, preferred_element_type=jnp.float32
    )
    grad_scale_two = jnp.sum(grad_hidden_two * normed_two, axis=1)
    grad_shift_two = jnp.sum(grad_hidden_two, axis=1)
    grad_after = grad_result + layer_back(
        normed_two, inverse_two, grad_hidden_two * (1.0 + scale_two)
    )
    grad_gate_one = jnp.sum(grad_after * attn_out, axis=1)
    grad_attn_float = grad_after * gate_one
    grad_attn = grad_attn_float.astype(jnp.bfloat16)
    grad_out_w = jnp.einsum("bsd,bse->de", mixed, grad_attn, preferred_element_type=jnp.float32)
    grad_out_b = jnp.sum(grad_attn_float, axis=(0, 1))
    grad_mixed = jnp.einsum(
        "bse,de->bsd", grad_attn, out_back, preferred_element_type=jnp.float32
    ).astype(jnp.bfloat16)
    grad_four = grad_mixed.reshape(latents, local_rows, HEADS, HEAD)
    mixed_four = mixed.reshape(latents, local_rows, HEADS, HEAD)
    row_inner = jnp.sum(
        grad_four.astype(jnp.float32) * mixed_four.astype(jnp.float32), axis=3
    ).transpose(0, 2, 1)

    def pair_grads(query_block, grad_block, lse_block, inner_block, key_block, value_block):
        scores = (
            jnp.einsum(
                "bqhd,bkhd->bhqk", query_block, key_block, preferred_element_type=jnp.float32
            )
            * scale_factor
        )
        probability = jnp.exp(scores - lse_block[..., None])
        grad_prob = jnp.einsum(
            "bqhd,bkhd->bhqk", grad_block, value_block, preferred_element_type=jnp.float32
        )
        grad_scores = (probability * (grad_prob - inner_block[..., None]) * scale_factor).astype(
            jnp.bfloat16
        )
        return (probability, grad_scores)

    query_start = jnp.zeros((latents, local_rows, HEADS, HEAD), jnp.float32)

    def back_block(grad_query, pair_items):
        key_block, value_block = pair_items
        probability, grad_scores = pair_grads(
            query_four, grad_four, log_total, row_inner, key_block, value_block
        )
        grad_value = jnp.einsum(
            "bhqk,bqhd->bkhd",
            probability.astype(jnp.bfloat16),
            grad_four,
            preferred_element_type=jnp.float32,
        )
        grad_query = grad_query + jnp.einsum(
            "bhqk,bkhd->bqhd", grad_scores, key_block, preferred_element_type=jnp.float32
        )
        grad_key = jnp.einsum(
            "bhqk,bqhd->bkhd", grad_scores, query_four, preferred_element_type=jnp.float32
        )
        pair_terms = jnp.concatenate(
            [
                grad_key.reshape(latents, local_rows, model_width),
                grad_value.reshape(latents, local_rows, model_width),
            ],
            axis=2,
        )
        return (grad_query, pair_terms)

    grad_query, stacked_terms = lax.scan(back_block, query_start, (key_blocks, value_blocks))
    key_terms = lax.psum_scatter(stacked_terms, "ctx", scatter_dimension=0, tiled=True)[0]
    grad_query_rows = grad_query.reshape(latents, local_rows, model_width)
    grad_projected = jnp.concatenate([grad_query_rows, key_terms], axis=2).astype(jnp.bfloat16)
    grad_qkv_w = jnp.einsum(
        "bsd,bse->de", hidden_one, grad_projected, preferred_element_type=jnp.float32
    )
    grad_qv_b = jnp.concatenate(
        [jnp.sum(grad_query_rows, axis=(0, 1)), jnp.sum(key_terms[..., model_width:], axis=(0, 1))]
    )
    grad_hidden_one = jnp.einsum(
        "bse,de->bsd", grad_projected, qkv_back, preferred_element_type=jnp.float32
    )
    grad_scale_one = jnp.sum(grad_hidden_one * normed_one, axis=1)
    grad_shift_one = jnp.sum(grad_hidden_one, axis=1)
    grad_input = (
        grad_after + layer_back(normed_one, inverse_one, grad_hidden_one * (1.0 + scale_one))
    ).astype(jnp.bfloat16)
    grad_mod = jnp.concatenate(
        [
            grad_shift_one,
            grad_scale_one,
            grad_gate_one,
            grad_shift_two,
            grad_scale_two,
            grad_gate_two,
        ],
        axis=1,
    )
    grad_ada_w = jnp.dot(cond_silu.astype(jnp.float32).T, grad_mod, precision=lax.Precision.HIGHEST)
    grad_ada_b = jnp.sum(grad_mod, axis=0)
    ada_back_term = jnp.dot(
        grad_mod, ada_back.astype(jnp.float32).T, precision=lax.Precision.HIGHEST
    )
    grad_cond_local = jax.vjp(jax.nn.silu, cond_float)[1](ada_back_term)[0]
    (
        share_ada_w,
        share_ada_b,
        share_qkv_w,
        share_qv_b,
        share_out_w,
        share_out_b,
        share_fc1_w,
        share_fc1_b,
        share_fc2_w,
        share_fc2_b,
    ) = (
        lax.psum_scatter(grad_ada_w, "fsdp", scatter_dimension=0, tiled=True),
        lax.psum_scatter(grad_ada_b, "fsdp", scatter_dimension=0, tiled=True),
        lax.psum_scatter(grad_qkv_w, "fsdp", scatter_dimension=0, tiled=True),
        lax.psum_scatter(grad_qv_b, "fsdp", scatter_dimension=0, tiled=True),
        lax.psum_scatter(grad_out_w, "fsdp", scatter_dimension=0, tiled=True),
        lax.psum_scatter(grad_out_b, "fsdp", scatter_dimension=0, tiled=True),
        lax.psum_scatter(grad_fc1_w, "fsdp", scatter_dimension=0, tiled=True),
        lax.psum_scatter(grad_fc1_b, "fsdp", scatter_dimension=0, tiled=True),
        lax.psum_scatter(grad_fc2_w, "fsdp", scatter_dimension=0, tiled=True),
        lax.psum_scatter(grad_fc2_b, "fsdp", scatter_dimension=0, tiled=True),
    )
    summed = lax.psum(
        (
            share_ada_w,
            share_ada_b,
            share_qkv_w,
            share_qv_b,
            share_out_w,
            share_out_b,
            share_fc1_w,
            share_fc1_b,
            share_fc2_w,
            share_fc2_b,
            grad_cond_local,
        ),
        "ctx",
    )
    return (
        result,
        grad_input,
        summed[10],
        summed[0],
        summed[1],
        summed[2],
        summed[3],
        summed[4],
        summed[5],
        summed[6],
        summed[7],
        summed[8],
        summed[9],
    )


def solution(mesh):
    return jax.shard_map(
        per_device,
        mesh=mesh,
        in_specs=(
            P("fsdp", "ctx", None),
            P("fsdp", None),
            P("fsdp", None),
            P("fsdp"),
            P("fsdp", None),
            P("fsdp"),
            P("fsdp", None),
            P("fsdp"),
            P("fsdp", None),
            P("fsdp"),
            P("fsdp", None),
            P("fsdp"),
            P("fsdp", "ctx", None),
        ),
        out_specs=(
            P("fsdp", "ctx", None),
            P("fsdp", "ctx", None),
            P("fsdp", None),
            P("fsdp", None),
            P("fsdp"),
            P("fsdp", None),
            P("fsdp"),
            P("fsdp", None),
            P("fsdp"),
            P("fsdp", None),
            P("fsdp"),
            P("fsdp", None),
            P("fsdp"),
        ),
        check_vma=False,
    )
```

profile of v0, /device:TPU:0, one launch (start us, length us, event | category | flops | bytes accessed | tf_op | source)
XLA Modules:
  0.0 564.0 jit_solution(625381980656653416)
XLA Ops:
  19.9 63.5 %all-reduce.15 = (bf16[2304]{0:T(1024)(128)(2,1)S(1)}, bf16[768]{0:T(1024)(128)(2,1)S(1)}, bf16[384]{0:T(512)(128)(2,1)S(1)}, bf16[384]{0:T(512)(128)(2,1)S(1)}, bf16[1536]{0:T(1024)(128)(2,1)S(1)}) all-reduce(bf16[2304]{0:T(1024)(128)(2,1)S(1)} %dynamic-update-slice, ...), channel_id=1, replica_groups=mesh['fsdp'=16,'ctx'=2] {'fsdp'}, use_global_device_ids=true, to_apply=%add | all-reduce | flops 5376 | bytes 21504
  84.6 18.3 %all_gather.47 = bf16[384,384]{1,0:T(8,128)(2,1)S(1)} all-gather(bf16[24,384]{1,0:T(8,128)(2,1)} %param.25), channel_id=1, replica_groups=mesh['fsdp'=16,'ctx'=2] {'fsdp'}, dimensions={0}, use_global_device_ids=true | all-gather | bytes 313344 | tf_op jit(solution)/shard_map/all_gather | solution.py:64
  102.9 23.7 %all_gather.43 = bf16[384,1152]{1,0:T(8,128)(2,1)S(1)} all-gather(bf16[24,1152]{1,0:T(8,128)(2,1)} %param.23), channel_id=1, replica_groups=mesh['fsdp'=16,'ctx'=2] {'fsdp'}, dimensions={0}, use_global_device_ids=true | all-gather | bytes 940032 | tf_op jit(solution)/shard_map/all_gather | solution.py:62
  126.6 1.8 convolution_reduce_fusion
  129.9 7.8 %all_gather.44 = bf16[1,512,384]{2,1,0:T(8,128)(2,1)S(1)} all-gather(bf16[1,256,384]{2,1,0:T(8,128)(2,1)S(1)} %slice.37), channel_id=1, replica_groups=mesh['fsdp'=16,'ctx'=2] {'ctx'}, dimensions={1}, use_global_device_ids=true | all-gather | bytes 589824 | tf_op jit(solution)/shard_map/all_gather | solution.py:89
  139.6 7.0 %all_gather.46 = bf16[1,512,384]{2,1,0:T(8,128)(2,1)S(1)} all-gather(bf16[1,256,384]{2,1,0:T(8,128)(2,1)S(1)} %get-tuple-element.339), channel_id=1, replica_groups=mesh['fsdp'=16,'ctx'=2] {'ctx'}, dimensions={1}, use_global_device_ids=true | all-gather | bytes 589824 | tf_op jit(solution)/shard_map/all_gather | solution.py:90
  147.5 1.8 transpose_reshape.7
  153.8 3.1 convolution_add_fusion
  157.0 3.2 fusion.112
  167.1 5.7 %while.39 = (s32[]{:T(128)}, f32[1,256,6,64]{1,3,2,0:T(8,128)S(1)}, f32[2,1,256,768]{2,3,1,0:T(8,128)}, bf16[2,1,256,6,64]{2,4,3,1,0:T(8,128)(2,1)S(1)}, bf16[1,...) while((s32[]{:T(128)}, f32[1,256,6,64]{1,3,2,0:T(8,128)S(1)}, ...), condition=%wide.region_14.15_spmd.clone, body=%wide.region_13.14_spmd.clone.sunk | while | flops 254803968 | bytes 11616399 | solution.py:242
  175.1 4.0 fusion.81
  180.2 2.0 fusion.71
  182.4 13.9 %reduce-scatter.11.cloned.1.call-done = f32[1,1,256,768]{2,3,1,0:T(8,128)} async-done(((f32[2,1,256,768]{2,3,1,0:T(8,128)}), f32[1,1,256,768]{2,3,1,0:T(8,128)}) %reduce-scatter.11.cloned.1.call-update) | async-done | bytes 786448 | tf_op jit(solution)/shard_map/reduce_scatter | solution.py:243
  197.6 1.8 fusion.75
  200.4 2.1 broadcast_multiply_fusion
  205.5 61.2 %all-reduce.12 = (f32[2304]{0:T(1024)S(1)}, f32[768]{0:T(1024)S(1)}, f32[384]{0:T(512)S(1)}, f32[1536]{0:T(1024)S(1)}, f32[384]{0:T(512)S(1)}) all-reduce(f32[2304]{0:T(1024)S(1)} %reduce.34, f32[768]{0:T(1024)S(1)} %pad_maximum_fusion.3, f32[384]{0:T(512)S(1)} %get-tuple-element.343, ...), channel_id=4, replica_groups=mesh['fsdp'=16,'ctx'=2] {'fsdp'}, use_global_device_ids=true, to_apply=%region_27.28.clone | all-reduce | flops 5376 | bytes 43008
  268.5 8.8 %all-reduce.13 = (f32[1,384]{1,0:T(1,128)}, f32[144]{0:T(256)}, f32[48]{0:T(128)}, f32[24,384]{1,0:T(8,128)}, f32[24]{0:T(128)}, /*index=5*/f32[96]{0:T(128)}, f32[24]{0:T(128)}) all-reduce(f32[1,384]{1,0:T(1,128)S(1)} %fusion.93, f32[144]{0:T(256)S(1)} %dynamic-slice.6, ...), channel_id=1, replica_groups=mesh['fsdp'=16,'ctx'=2] {'ctx'}, use_global_device_ids=true, to_apply=%region_24.25 | all-reduce | flops 9936 | bytes 79488 | tf_op jit(solution)/shard_map/psum | solution.py:300
  277.3 42.5 %reduce-scatter.17.cloned.1.call-done = f32[96,384]{1,0:T(8,128)} async-done(((f32[1536,384]{1,0:T(8,128)}), f32[96,384]{1,0:T(8,128)}) %reduce-scatter.17.cloned.1.call-update) | async-done | bytes 147472 | tf_op jit(solution)/shard_map/reduce_scatter | solution.py:297
  319.8 66.0 %reduce-scatter.15.cloned.1.call-done = f32[24,1536]{1,0:T(8,128)} async-done(((f32[384,1536]{1,0:T(8,128)}), f32[24,1536]{1,0:T(8,128)}) %reduce-scatter.15.cloned.1.call-update) | async-done | bytes 147472 | tf_op jit(solution)/shard_map/reduce_scatter | solution.py:295
  385.8 62.0 %reduce-scatter.19.cloned.1.call-done = f32[24,1152]{1,0:T(8,128)} async-done(((f32[384,1152]{1,0:T(8,128)}), f32[24,1152]{1,0:T(8,128)}) %reduce-scatter.19.cloned.1.call-update) | async-done | bytes 110608
  447.8 70.8 %reduce-scatter.13.cloned.1.call-done = f32[24,2304]{1,0:T(8,128)} async-done(((f32[384,2304]{1,0:T(8,128)}), f32[24,2304]{1,0:T(8,128)}) %reduce-scatter.13.cloned.1.call-update) | async-done | bytes 221200 | tf_op jit(solution)/shard_map/reduce_scatter | solution.py:289
  518.7 1.9 fusion.60
  520.6 30.3 %all-reduce.18.cloned.1.call-done = (f32[24,2304]{1,0:T(8,128)}, f32[24,1152]{1,0:T(8,128)}, f32[24,1536]{1,0:T(8,128)}, f32[96,384]{1,0:T(8,128)}) async-done(((f32[24,2304]{1,0:T(8,128)}, f32[24,1152]{1,0:T(8,128)}, f32[24,1536]{1,0:T(8,128)}, f32[96,384]{1,0:T(8,128)}), (f32[24,2304]{1,0:T(8,128)}, f32[24,1152]{1,0:T(8,128)}, f32[24,1536]{1,0:T(8,128)}, ...) | async-done | bytes 626704 | tf_op jit(solution)/shard_map/psum | solution.py:300
  550.8 1.6 copy.93
  (189 shorter events, 47.3 us)
Async XLA Ops:
  7.2 119.4 %copy-start.22 = (bf16[1,384]{1,0:T(2,128)(2,1)S(1)}, bf16[1,384]{1,0:T(2,128)(2,1)}, u32[]{:S(2)}) copy-start(bf16[1,384]{1,0:T(2,128)(2,1)} %param.20) | copy-start | bytes 2308
  7.2 119.4 %all-gather.4.cloned.1.call-start = ((), (), s32[]{:S(2)}) async-start(), calls=%async_computation.6 | async-start | bytes 1880064 | tf_op jit(solution)/shard_map/all_gather | solution.py:60
  7.9 145.9 %all-gather.6.cloned.1.call-start = ((), (), s32[]{:S(2)}) async-start(), calls=%async_computation.7 | async-start | bytes 1253376 | tf_op jit(solution)/shard_map/all_gather | solution.py:66
  8.7 148.3 %all-gather.8.cloned.1.call-start = ((), (), s32[]{:S(2)}) async-start(), calls=%async_computation.8 | async-start | bytes 1253376 | tf_op jit(solution)/shard_map/all_gather | solution.py:68
  9.4 186.9 %reduce-scatter.11.cloned.1.call-start = ((), (), s32[]{:S(2)}) async-start(), calls=%async_computation.9 | async-start | bytes 2359296 | tf_op jit(solution)/shard_map/reduce_scatter | solution.py:243
  14.5 114.6 %copy-start.15 = (f32[256]{0:T(256)}, f32[256]{0:T(256)S(1)}, u32[]{:S(2)}) copy-start(f32[256]{0:T(256)S(1)} %broadcast_multiply_fusion.6) | copy-start | bytes 3076
  15.7 113.4 %copy-start.20 = (f32[256]{0:T(256)}, f32[256]{0:T(256)S(1)}, u32[]{:S(2)}) copy-start(f32[256]{0:T(256)S(1)} %add_rsqrt_fusion.1) | copy-start | bytes 3076
  84.0 45.1 %copy-start = (bf16[1,256,384]{2,1,0:T(8,128)(2,1)S(1)}, bf16[1,256,384]{2,1,0:T(8,128)(2,1)}, u32[]{:S(2)}) copy-start(bf16[1,256,384]{2,1,0:T(8,128)(2,1)} %param.19) | copy-start | bytes 589828
  102.9 49.6 %copy-start.2 = (bf16[384,384]{1,0:T(8,128)(2,1)}, bf16[384,384]{1,0:T(8,128)(2,1)S(1)}, u32[]{:S(2)}) copy-start(bf16[384,384]{1,0:T(8,128)(2,1)S(1)} %all_gather.47) | copy-start | bytes 884740
  151.8 5.1 copy-start.5
  153.8 3.1 copy-start.26
  153.8 3.1 copy-start.28
  156.9 3.3 copy-start.10
  157.0 4.2 copy-start.29
  172.8 95.7 %reduce-scatter.21.cloned.1.call-start = ((), (), s32[]{:S(2)}) async-start(), calls=%async_computation.14 | async-start | bytes 626688
  174.8 145.0 %reduce-scatter.17.cloned.1.call-start = ((), (), s32[]{:S(2)}) async-start(), calls=%async_computation.12 | async-start | bytes 2506752 | tf_op jit(solution)/shard_map/reduce_scatter | solution.py:297
  179.1 206.7 %reduce-scatter.15.cloned.1.call-start = ((), (), s32[]{:S(2)}) async-start(), calls=%async_computation.11 | async-start | bytes 2506752 | tf_op jit(solution)/shard_map/reduce_scatter | solution.py:295
  182.2 15.3 %copy-start.16 = (f32[256]{0:T(256)S(1)}, f32[256]{0:T(256)}, u32[]{:S(2)}) copy-start(f32[256]{0:T(256)} %copy-done.15) | copy-start | bytes 3076
  182.2 15.3 %copy-start.18 = (f32[384]{0:T(512)S(1)}, f32[384]{0:T(512)}, u32[]{:S(2)}) copy-start(f32[384]{0:T(512)} %copy-done.17) | copy-start | bytes 4612
  182.2 15.3 %copy-start.21 = (f32[256]{0:T(256)S(1)}, f32[256]{0:T(256)}, u32[]{:S(2)}) copy-start(f32[256]{0:T(256)} %copy-done.20) | copy-start | bytes 3076
  182.3 265.6 %reduce-scatter.19.cloned.1.call-start = ((), (), s32[]{:S(2)}) async-start(), calls=%async_computation.13 | async-start | bytes 1880064
  199.4 319.3 %reduce-scatter.13.cloned.1.call-start = ((), (), s32[]{:S(2)}) async-start(), calls=%async_computation.10 | async-start | bytes 3760128 | tf_op jit(solution)/shard_map/reduce_scatter | solution.py:289
  202.4 64.6 %copy-start.1 = (bf16[384,2304]{1,0:T(8,128)(2,1)S(1)}, bf16[384,2304]{1,0:T(8,128)(2,1)}, u32[]{:S(2)}) copy-start(bf16[384,2304]{1,0:T(8,128)(2,1)} %all-gather.4.cloned.1.call-done) | copy-start | bytes 5308420
  202.4 348.4 %all-reduce.18.cloned.1.call-start = ((), (), s32[]{:S(2)}) async-start(), calls=%async_computation.15 | async-start | bytes 1253376 | tf_op jit(solution)/shard_map/psum | solution.py:300
  (17 other events, 28.8 us)
Sparse Core Ops, SparseCore 0:
  10.2 43.1 all-gather.3
  55.7 37.3 all-gather.5
  95.3 37.4 all-gather.7
  172.9 23.3 reduce-scatter.10
  199.7 54.0 reduce-scatter.20
  257.5 62.2 reduce-scatter.16
  323.6 62.1 reduce-scatter.14
  389.6 58.1 reduce-scatter.18
  451.7 66.9 reduce-scatter.12
  521.0 29.7 all-reduce.17
where the time goes:
time: 565 us; the launch traced here: 564 us
  waiting for transfers between devices  288 us (51%)
  blocking collectives  190 us (34%)
  matrix products  30 us (5%)
  local copies, waits for them, and re-layouts  21.8 us (4%)
  between operations  20.1 us (4%)
  other arithmetic  13.4 us (2%)
    unnamed x2, blocking collectives  125 us
    reduce_scatter x1, waiting for transfers between devices, per_device(): lax.psum_scatter(grad_ada_w, 'fsdp', scatter_dimension=0, tiled=True)  70.8 us
    reduce_scatter x1, waiting for transfers between devices, per_device(): lax.psum_scatter(grad_fc1_w, 'fsdp', scatter_dimension=0, tiled=True)  66 us
    unnamed x12, waiting for transfers between devices  64.2 us
    reduce_scatter x1, waiting for transfers between devices, per_device(): lax.psum_scatter(grad_fc2_w, 'fsdp', scatter_dimension=0, tiled=True)  42.5 us
    psum x1, waiting for transfers between devices, per_device(): lax.psum((share_ada_w, share_ada_b, share_qkv_w, share_qv_b, share_out_w,...  30.3 us
    all_gather x1, blocking collectives, per_device(): lax.all_gather(qkv_weight, 'fsdp', axis=0, tiled=True)  23.7 us
    all_gather x1, blocking collectives, per_device(): lax.all_gather(out_weight, 'fsdp', axis=0, tiled=True)  18.3 us
  transfers between devices with their start and end apart: 10, of which 6 were waited for; matrix products, arithmetic and copies ran while one was open for 7% of the time, Pallas kernels for 0%

commit v1 on v0

v1 whole, which is shorter than its diff:
```python
from functools import partial

import jax
import jax.numpy as jnp
from jax import lax
from jax.experimental import pallas as pl
from jax.experimental.pallas import tpu as pltpu
from jax.sharding import PartitionSpec as P

HEADS = 6
HEAD = 64
MESH = pl.DeviceIdType.MESH
F32 = jnp.float32
BF16 = jnp.bfloat16


epsilon = 1e-06


def layer_stats(values):
    centered = values - jnp.mean(values, axis=-1, keepdims=True)
    inverse = lax.rsqrt(jnp.mean(centered * centered, axis=-1, keepdims=True) + epsilon)
    return (centered * inverse, inverse)


def layer_back(normed, inverse, grad_normed):
    mean_grad = jnp.mean(grad_normed, axis=-1, keepdims=True)
    mean_prod = jnp.mean(grad_normed * normed, axis=-1, keepdims=True)
    return inverse * (grad_normed - mean_grad - normed * mean_prod)


def gelu_back(hidden, grad_output):
    return jax.vjp(partial(jax.nn.gelu, approximate=True), hidden)[1](grad_output)[0]


def matmul(left, right):
    return jnp.dot(left, right, preferred_element_type=F32)


def matmul_nt(left, right):
    return lax.dot_general(left, right, (((1,), (1,)), ((), ())), preferred_element_type=F32)


def matmul_tn(left, right):
    return lax.dot_general(left, right, (((0,), (0,)), ((), ())), preferred_element_type=F32)


def flip(index, mask):
    return index + mask - 2 * mask * ((index // mask) % 2)


def loop(count, body):
    def step(i, carry):
        body(i)
        return carry

    lax.fori_loop(0, count, step, 0)


def remote(src, dst, send, recv, **device):
    return pltpu.make_async_remote_copy(
        src_ref=src, dst_ref=dst, send_sem=send, recv_sem=recv,
        device_id=device, device_id_type=MESH,
    )


def meet(n, c, me, row):
    barrier = pltpu.get_barrier_semaphore()

    def greet_fsdp(k):
        pl.semaphore_signal(
            barrier, inc=1, device_id={"fsdp": (me + 1 + k) % n}, device_id_type=MESH
        )

    def greet_ctx(k):
        pl.semaphore_signal(
            barrier, inc=1, device_id={"ctx": (row + 1 + k) % c}, device_id_type=MESH
        )

    loop(n - 1, greet_fsdp)
    loop(c - 1, greet_ctx)
    pl.semaphore_wait(barrier, n + c - 2)


def gather_kernel(
    n, c,
    qkv, out, fc1, fc2, tok, cond, ada, ada_bias, small,
    qkv_all, out_all, fc1_all, fc2_all, tok_all, cond_all, mod, small_all,
    part, mod_all,
    send_w, recv_w, send_t, recv_t, send_c, recv_c, send_m, recv_m, send_s, recv_s,
):
    me, row = lax.axis_index("fsdp"), lax.axis_index("ctx")
    own = (qkv, out, fc1, fc2)
    full = (qkv_all, out_all, fc1_all, fc2_all)
    stages = n.bit_length() - 1
    meet(n, c, me, row)

    def cond_copy(to, sender):
        return remote(
            cond.at[to], cond_all.at[sender], send_c.at[to], recv_c.at[sender], fsdp=to
        )

    def small_copy(to, sender):
        return remote(small, small_all.at[sender], send_s.at[to], recv_s.at[sender], fsdp=to)

    def mod_copy(to, sender):
        return remote(part.at[to], mod_all.at[sender], send_m.at[to], recv_m.at[sender], fsdp=to)

    def tok_copy(to, sender):
        return remote(tok, tok_all.at[sender], send_t.at[to], recv_t.at[sender], ctx=to)

    def weight_copy(w, s, block, mine):
        return remote(
            own[w] if mine else full[w].at[block],
            full[w].at[block],
            send_w.at[w, s, block],
            recv_w.at[w, block],
            fsdp=flip(me, n >> (s + 1)),
        )

    def others(body):
        loop(n - 1, lambda k: body((me + 1 + k) % n))

    def siblings(body):
        loop(c - 1, lambda k: body((row + 1 + k) % c))

    others(lambda to: cond_copy(to, me).start())
    for w in range(4):
        for s in range(stages):
            weight_copy(w, s, me, True).start()
    others(lambda to: small_copy(to, me).start())
    siblings(lambda to: tok_copy(to, row).start())
    for w in range(4):
        full[w][me] = own[w][...]
    tok_all[row] = tok[...]
    small_all[me] = small[...]
    cond_all[me] = cond[me]
    others(lambda peer: cond_copy(peer, peer).wait_recv())
    lane = lax.broadcasted_iota(jnp.int32, cond_all.shape[1:], 1)
    columns = jnp.zeros(cond_all.shape[1:], F32)
    for i in range(n):
        columns = jnp.where(lane == i, cond_all[i], columns)
    partial_mod = matmul_tn(columns.astype(BF16), ada[...])
    for i in range(n):
        part[i] = partial_mod[i : i + 1, :] + ada_bias[...]
    others(lambda to: mod_copy(to, me).start())
    mod_all[me] = part[me]

    for s in range(stages):
        mask = n >> (s + 1)
        origin = flip(me, mask) % (2 * mask)

        def arrived(t, s=s, mask=mask, origin=origin):
            block = origin + t * (2 * mask)
            for w in range(4):
                weight_copy(w, s, block, False).wait_recv()
                for later in range(s + 1, stages):
                    weight_copy(w, later, block, False).start()

        loop(1 << s, arrived)

    others(lambda peer: mod_copy(peer, peer).wait_recv())
    total = mod_all[0]
    for i in range(1, n):
        total = total + mod_all[i]
    mod[...] = total
    others(lambda peer: small_copy(peer, peer).wait_recv())
    siblings(lambda peer: tok_copy(peer, peer).wait_recv())
    for s in range(stages):
        mask = n >> (s + 1)

        def left(t, s=s, mask=mask):
            block = me % (2 * mask) + t * (2 * mask)
            for w in range(4):
                weight_copy(w, s, block, False).wait_send()

        loop(1 << s, left)
    others(lambda to: cond_copy(to, me).wait_send())
    others(lambda to: small_copy(to, me).wait_send())
    others(lambda to: mod_copy(to, me).wait_send())
    siblings(lambda to: tok_copy(to, row).wait_send())


def vmem(count):
    return [pl.BlockSpec(memory_space=pltpu.VMEM)] * count


def gather(n, c, qkv, out, fc1, fc2, tok, cond, ada, ada_bias, small):
    stages = n.bit_length() - 1
    shape = jax.ShapeDtypeStruct
    dma = pltpu.SemaphoreType.DMA
    return pl.pallas_call(
        partial(gather_kernel, n, c),
        out_shape=[shape((n, *w.shape), BF16) for w in (qkv, out, fc1, fc2)]
        + [
            shape((c, *tok.shape), BF16),
            shape(cond.shape, F32),
            shape(ada_bias.shape, F32),
            shape((n, *small.shape), F32),
        ],
        in_specs=vmem(9),
        out_specs=vmem(8),
        scratch_shapes=[
            pltpu.VMEM((n, *ada_bias.shape), F32),
            pltpu.VMEM((n, *ada_bias.shape), F32),
            dma((4, stages, n)), dma((4, n)),
            dma((c,)), dma((c,)), dma((n,)), dma((n,)), dma((n,)), dma((n,)), dma((n,)), dma((n,)),
        ],
        compiler_params=pltpu.CompilerParams(collective_id=0, has_side_effects=True),
        name="gather",
    )(qkv, out, fc1, fc2, tok, cond, ada, ada_bias, small)


def reduce_kernel(
    n, c,
    qkv, out, fc1, fc2, bias, gm, ada,
    qkv_sum, out_sum, fc1_sum, fc2_sum, bias_sum, gm_all, back_all,
    *scratch,
):
    stages = n.bit_length() - 1
    me, row = lax.axis_index("fsdp"), lax.axis_index("ctx")
    given = (qkv, out, fc1, fc2, bias)
    sums = (qkv_sum, out_sum, fc1_sum, fc2_sum, bias_sum)
    arrays = len(given)
    incoming = [scratch[w * stages : (w + 1) * stages] for w in range(arrays)]
    scratch = scratch[arrays * stages :]
    kept = [scratch[w * stages : (w + 1) * stages] for w in range(arrays)]
    scratch = scratch[arrays * stages :]
    shares, scratch = scratch[:arrays], scratch[arrays:]
    (gm_ctx, gm_mine, back, send_r, recv_r, send_x, recv_x, send_g, recv_g, send_f, recv_f,
     send_b, recv_b) = scratch
    meet(n, c, me, row)

    def others(body):
        loop(n - 1, lambda k: body((me + 1 + k) % n))

    def siblings(body):
        loop(c - 1, lambda k: body((row + 1 + k) % c))

    def ctx_gm(to, sender):
        return remote(gm, gm_ctx.at[sender], send_g.at[to], recv_g.at[sender], ctx=to)

    def fsdp_gm(to, sender):
        return remote(gm_mine, gm_all.at[sender], send_f.at[to], recv_f.at[sender], fsdp=to)

    def back_copy(to, sender):
        return remote(back.at[to], back_all.at[sender], send_b.at[to], recv_b.at[sender], fsdp=to)

    def share_copy(w, to, sender):
        return remote(
            shares[w].at[row], shares[w].at[sender], send_x.at[w, to], recv_x.at[w, sender], ctx=to
        )

    def bit(s):
        return (me // (1 << s)) % 2

    def source(w, s):
        return given[w] if s == 0 else kept[w][s - 1]

    def halve(w, s, j):
        return remote(
            source(w, s).at[2 * j + 1 - bit(s)],
            incoming[w][s].at[j],
            send_r.at[w, s, j],
            recv_r.at[w, s, j],
            fsdp=flip(me, 1 << s),
        )

    siblings(lambda to: ctx_gm(to, row).start())

    def send_all(s, base, step, count):
        def body(t):
            for w in range(arrays):
                halve(w, s, base + step * t).start()

        loop(count, body)

    send_all(0, 1 - bit(1), 2, n // 4)
    send_all(0, bit(1), 2, n // 4)

    gm_ctx[row] = gm[...]
    siblings(lambda peer: ctx_gm(peer, peer).wait_recv())
    total = gm_ctx[0]
    for i in range(1, c):
        total = total + gm_ctx[i]
    gm_mine[...] = total
    gm_all[me] = total
    others(lambda to: fsdp_gm(to, me).start())

    def backward():
        others(lambda peer: fsdp_gm(peer, peer).wait_recv())
        rows = lax.broadcasted_iota(jnp.int32, (n, gm.shape[1]), 0)
        stacked = jnp.zeros((n, gm.shape[1]), F32)
        for i in range(n):
            stacked = jnp.where(rows == i, jnp.broadcast_to(gm_all[i], stacked.shape), stacked)
        product = lax.dot_general(
            stacked, ada[...], (((1,), (1,)), ((), ())),
            preferred_element_type=F32, precision=lax.Precision.HIGHEST,
        )
        for i in range(n):
            back[i] = product[i : i + 1, :]
        others(lambda to: back_copy(to, me).start())
        back_all[me] = back[me]

    def add(w, s, j):
        halve(w, s, j).wait_recv()
        value = source(w, s)[2 * j + bit(s)].astype(F32) + incoming[w][s][j].astype(F32)
        if s == stages - 1:
            shares[w][row] = value.astype(given[w].dtype)
        else:
            kept[w][s][j] = value.astype(given[w].dtype)

    for s in range(stages):
        if s == stages - 1:
            for w in range(arrays):
                add(w, s, 0)
                siblings(lambda to, w=w: share_copy(w, to, row).start())
            continue

        def first(t, s=s):
            j = 2 * t + 1 - bit(s + 1)
            for w in range(arrays):
                add(w, s, j)
                halve(w, s + 1, t).start()

        def second(t, s=s):
            for w in range(arrays):
                add(w, s, 2 * t + bit(s + 1))

        loop(n >> (s + 2), first)
        loop(n >> (s + 2), second)
        if s == 0:
            backward()

    for w in range(arrays):
        siblings(lambda peer, w=w: share_copy(w, peer, peer).wait_recv())
        value = shares[w][0].astype(F32)
        for i in range(1, c):
            value = value + shares[w][i].astype(F32)
        sums[w][...] = value
    others(lambda peer: back_copy(peer, peer).wait_recv())

    siblings(lambda to: ctx_gm(to, row).wait_send())
    others(lambda to: fsdp_gm(to, me).wait_send())
    others(lambda to: back_copy(to, me).wait_send())
    for s in range(stages):

        def sent(j, s=s):
            for w in range(arrays):
                halve(w, s, j).wait_send()

        loop(n >> (s + 1), sent)
    for w in range(arrays):
        siblings(lambda to, w=w: share_copy(w, to, row).wait_send())


def reduce(n, c, qkv, out, fc1, fc2, bias, gm, ada):
    stages = n.bit_length() - 1
    shape = jax.ShapeDtypeStruct
    dma = pltpu.SemaphoreType.DMA
    given = (qkv, out, fc1, fc2, bias)
    halves = [
        pltpu.VMEM((n >> (s + 1), *w.shape[1:]), w.dtype) for w in given for s in range(stages)
    ]
    return pl.pallas_call(
        partial(reduce_kernel, n, c),
        out_shape=[shape(w.shape[1:], F32) for w in given]
        + [shape((n, *gm.shape), F32), shape((n, 1, ada.shape[0]), F32)],
        in_specs=vmem(7),
        out_specs=vmem(7),
        scratch_shapes=halves
        + halves
        + [pltpu.VMEM((c, *w.shape[1:]), w.dtype) for w in given]
        + [
            pltpu.VMEM((c, *gm.shape), F32),
            pltpu.VMEM(gm.shape, F32),
            pltpu.VMEM((n, 1, ada.shape[0]), F32),
            dma((5, stages, n // 2)), dma((5, stages, n // 2)),
            dma((5, c)), dma((5, c)), dma((c,)), dma((c,)),
            dma((n,)), dma((n,)), dma((n,)), dma((n,)),
        ],
        compiler_params=pltpu.CompilerParams(collective_id=1, has_side_effects=True),
        name="reduce",
    )(qkv, out, fc1, fc2, bias, gm, ada)


def per_device(
    n, c,
    tokens, condition,
    ada_weight, ada_bias, qkv_weight, qv_bias, out_weight, out_bias,
    fc1_weight, fc1_bias, fc2_weight, fc2_bias,
    cotangent,
):
    latents, local_rows, width = tokens.shape
    me, row = lax.axis_index("fsdp"), lax.axis_index("ctx")
    scale_factor = HEAD ** (-0.5)
    tok = tokens[0]
    slice_rows = ada_weight.shape[0]
    cond_float = condition.astype(F32)
    cond_silu = jax.nn.silu(cond_float).astype(BF16)
    cond_columns = jnp.broadcast_to(
        cond_silu.astype(F32).reshape(n, slice_rows, 1), (n, slice_rows, 128)
    )
    bias_row = lax.dynamic_update_slice(
        jnp.zeros((1, ada_bias.shape[0] * n), F32),
        ada_bias.astype(F32)[None, :],
        (0, me * ada_bias.shape[0]),
    )
    biases = jnp.concatenate([qv_bias, out_bias, fc1_bias, fc2_bias]).astype(F32)
    small = jnp.pad(biases, (0, 256 - biases.shape[0]))[None, :]
    qkv_all, out_all, fc1_all, fc2_all, tok_all, cond_all, modulation, small_all = gather(
        n, c, qkv_weight, out_weight, fc1_weight, fc2_weight, tok, cond_columns,
        ada_weight, bias_row, small,
    )
    qkv_full = qkv_all.reshape(-1, qkv_weight.shape[1])
    out_full = out_all.reshape(-1, width)
    fc1_full = fc1_all.reshape(-1, fc1_weight.shape[1])
    fc2_full = fc2_all.reshape(-1, width)
    pieces, start = [], 0
    for piece in (qv_bias, out_bias, fc1_bias, fc2_bias):
        pieces.append(small_all[:, 0, start : start + piece.shape[0]].reshape(1, -1))
        start += piece.shape[0]
    qv_full, out_bias_full, fc1_bias_full, fc2_bias_full = pieces
    shift_one, scale_one, gate_one, shift_two, scale_two, gate_two = jnp.split(
        modulation, 6, axis=1
    )
    order = [lax.rem(row + k, c) for k in range(c)]
    rotated = jnp.concatenate([tok] + [tok_all[i] for i in order[1:]], axis=0)
    residual_all = rotated.astype(F32)
    normed_all, inverse_all = layer_stats(residual_all)
    hidden_all = (normed_all * (1.0 + scale_one) + shift_one).astype(BF16)
    residual = residual_all[:local_rows]
    normed_one, inverse_one = normed_all[:local_rows], inverse_all[:local_rows]
    hidden_one = hidden_all[:local_rows]
    queries = (matmul(hidden_one, qkv_full[:, :width]) + qv_full[:, :width]).astype(BF16)
    keys = matmul(hidden_all, qkv_full[:, width : 2 * width]).astype(BF16)
    values = (matmul(hidden_all, qkv_full[:, 2 * width :]) + qv_full[:, width:]).astype(BF16)

    def head(array, h):
        return array[:, h * HEAD : (h + 1) * HEAD]

    probabilities, mixed_heads = [], []
    for h in range(HEADS):
        scores = matmul_nt(head(queries, h), head(keys, h)) * scale_factor
        raised = jnp.exp(scores - jnp.max(scores, axis=1, keepdims=True))
        probability = raised / jnp.sum(raised, axis=1, keepdims=True)
        probabilities.append(probability)
        mixed_heads.append(matmul(probability.astype(BF16), head(values, h)))
    mixed = jnp.concatenate(mixed_heads, axis=1).astype(BF16)
    attn_out = matmul(mixed, out_full) + out_bias_full
    after_attn = residual + gate_one * attn_out
    normed_two, inverse_two = layer_stats(after_attn)
    hidden_two = (normed_two * (1.0 + scale_two) + shift_two).astype(BF16)
    pre_act = matmul(hidden_two, fc1_full) + fc1_bias_full
    activated = jax.nn.gelu(pre_act, approximate=True).astype(BF16)
    mlp_out = matmul(activated, fc2_full) + fc2_bias_full
    result = (after_attn + gate_two * mlp_out).astype(BF16)

    grad_result = cotangent[0].astype(F32)
    grad_gate_two = jnp.sum(grad_result * mlp_out, axis=0, keepdims=True)
    grad_mlp_float = grad_result * gate_two
    grad_mlp = grad_mlp_float.astype(BF16)
    grad_fc2_w = matmul_tn(activated, grad_mlp)
    grad_fc2_b = jnp.sum(grad_mlp_float, axis=0)
    grad_pre = gelu_back(pre_act, matmul_nt(grad_mlp, fc2_full))
    grad_pre_half = grad_pre.astype(BF16)
    grad_fc1_w = matmul_tn(hidden_two, grad_pre_half)
    grad_fc1_b = jnp.sum(grad_pre, axis=0)
    grad_hidden_two = matmul_nt(grad_pre_half, fc1_full)
    grad_scale_two = jnp.sum(grad_hidden_two * normed_two, axis=0, keepdims=True)
    grad_shift_two = jnp.sum(grad_hidden_two, axis=0, keepdims=True)
    grad_after = grad_result + layer_back(
        normed_two, inverse_two, grad_hidden_two * (1.0 + scale_two)
    )
    grad_gate_one = jnp.sum(grad_after * attn_out, axis=0, keepdims=True)
    grad_attn_float = grad_after * gate_one
    grad_attn = grad_attn_float.astype(BF16)
    grad_out_w = matmul_tn(mixed, grad_attn)
    grad_out_b = jnp.sum(grad_attn_float, axis=0)
    grad_mixed = matmul_nt(grad_attn, out_full).astype(BF16)
    grad_q, grad_k, grad_v = [], [], []
    for h in range(HEADS):
        grad_head = head(grad_mixed, h)
        inner = jnp.sum(
            grad_head.astype(F32) * head(mixed, h).astype(F32), axis=1, keepdims=True
        )
        grad_prob = matmul_nt(grad_head, head(values, h))
        grad_scores = (probabilities[h] * (grad_prob - inner) * scale_factor).astype(BF16)
        grad_q.append(matmul(grad_scores, head(keys, h)))
        grad_k.append(matmul_tn(grad_scores, head(queries, h)))
        grad_v.append(matmul_tn(probabilities[h].astype(BF16), grad_head))
    grad_query = jnp.concatenate(grad_q, axis=1)
    grad_value = jnp.concatenate(grad_v, axis=1)
    grad_qv_b = jnp.concatenate([jnp.sum(grad_query, axis=0), jnp.sum(grad_value, axis=0)])
    grad_kv = jnp.concatenate(grad_k + grad_v, axis=1).astype(BF16)
    grad_query = grad_query.astype(BF16)
    grad_hidden_kv = matmul_nt(grad_kv, qkv_full[:, width:])
    grad_hidden_one = grad_hidden_kv[:local_rows] + matmul_nt(grad_query, qkv_full[:, :width])
    for k in range(1, c):
        sent = grad_hidden_kv[k * local_rows : (k + 1) * local_rows].astype(BF16)
        moved = lax.ppermute(sent, "ctx", [(i, (i + k) % c) for i in range(c)])
        grad_hidden_one = grad_hidden_one + moved.astype(F32)
    grad_qkv_w = jnp.concatenate(
        [matmul_tn(hidden_one, grad_query), matmul_tn(hidden_all, grad_kv)], axis=1
    )
    grad_scale_one = jnp.sum(grad_hidden_one * normed_one, axis=0, keepdims=True)
    grad_shift_one = jnp.sum(grad_hidden_one, axis=0, keepdims=True)
    grad_input = (
        grad_after + layer_back(normed_one, inverse_one, grad_hidden_one * (1.0 + scale_one))
    ).astype(BF16)
    grad_mod = jnp.concatenate(
        [grad_shift_one, grad_scale_one, grad_gate_one, grad_shift_two, grad_scale_two,
         grad_gate_two],
        axis=1,
    )
    bias_grads = jnp.concatenate(
        [g.reshape(n, -1) for g in (grad_qv_b, grad_out_b, grad_fc1_b, grad_fc2_b)], axis=1
    )
    bias_grads = jnp.pad(bias_grads, ((0, 0), (0, 1024 - bias_grads.shape[1])))
    ada_rows = jnp.pad(ada_weight.astype(F32), ((0, 128 - slice_rows), (0, 0)))
    qkv_sum, out_sum, fc1_sum, fc2_sum, bias_sum, mod_all, back_all = reduce(
        n, c,
        grad_qkv_w.astype(BF16).reshape(qkv_all.shape),
        grad_out_w.astype(BF16).reshape(out_all.shape),
        grad_fc1_w.astype(BF16).reshape(fc1_all.shape),
        grad_fc2_w.astype(BF16).reshape(fc2_all.shape),
        bias_grads.reshape(n, 8, 128), grad_mod, ada_rows,
    )
    mod_all = mod_all[:, 0, :]
    grad_ada_w = lax.dot_general(
        cond_all[:, :, 0], mod_all, (((0,), (0,)), ((), ())),
        precision=lax.Precision.HIGHEST, preferred_element_type=F32,
    )
    grad_ada_b = jnp.sum(
        lax.dynamic_slice(mod_all, (0, me * ada_bias.shape[0]), (n, ada_bias.shape[0])), axis=0
    )
    ada_back_term = back_all[:, 0, :slice_rows].reshape(1, -1)
    grad_cond = jax.vjp(jax.nn.silu, cond_float)[1](ada_back_term)[0]
    flat, parts, start = bias_sum.reshape(-1), [], 0
    for piece in (qv_bias, out_bias, fc1_bias, fc2_bias):
        parts.append(flat[start : start + piece.shape[0]])
        start += piece.shape[0]
    return (
        result[None], grad_input[None], grad_cond,
        grad_ada_w, grad_ada_b,
        qkv_sum, parts[0], out_sum, parts[1], fc1_sum, parts[2], fc2_sum, parts[3],
    )


def solution(mesh):
    n, c = mesh.shape["fsdp"], mesh.shape["ctx"]
    return jax.shard_map(
        partial(per_device, n, c),
        mesh=mesh,
        in_specs=(
            P("fsdp", "ctx", None),
            P("fsdp", None),
            P("fsdp", None),
            P("fsdp"),
            P("fsdp", None),
            P("fsdp"),
            P("fsdp", None),
            P("fsdp"),
            P("fsdp", None),
            P("fsdp"),
            P("fsdp", None),
            P("fsdp"),
            P("fsdp", "ctx", None),
        ),
        out_specs=(
            P("fsdp", "ctx", None),
            P("fsdp", "ctx", None),
            P("fsdp", None),
            P("fsdp", None),
            P("fsdp"),
            P("fsdp", None),
            P("fsdp"),
            P("fsdp", None),
            P("fsdp"),
            P("fsdp", None),
            P("fsdp"),
            P("fsdp", None),
            P("fsdp"),
        ),
        check_vma=False,
    )
```

time: 565 us -> 172 us (0.30)
  waiting for transfers between devices: 288 us -> 0.01 us
  blocking collectives: 190 us -> 0 us
  Pallas kernels: 0 us -> 92.6 us
  between operations: 20.1 us -> 1.73 us
  matrix products: 30 us -> 40 us
    reduce_scatter x4 -> x0, waiting for transfers between devices: 193 us -> none  [the longest x1 70.8 us: per_device(): lax.psum_scatter(grad_ada_w, 'fsdp', scatter_dimension=0, tiled=True)]
    unnamed x2 -> x0, blocking collectives: 125 us -> none
    pallas_call x0 -> x2, Pallas kernels: none -> 92.6 us  [the longest x1 49.2 us: reduce(): pl.pallas_call(partial(reduce_kernel, n, c), out_shape=[shape(w.shape[1:]...]
    unnamed x12 -> x0, waiting for transfers between devices: 64.2 us -> none
    all_gather x4 -> x0, blocking collectives: 56.8 us -> none  [the longest x1 23.7 us: per_device(): lax.all_gather(qkv_weight, 'fsdp', axis=0, tiled=True)]
    psum x1 -> x0, waiting for transfers between devices: 30.3 us -> none  [per_device(): lax.psum((share_ada_w, share_ada_b, share_qkv_w, share_qv_b, share_out_w,...]
    unnamed x89 -> x159, local copies, waits for them, and re-layouts: 17.4 us -> 4.78 us
    dot_general x28 -> x53, matrix products: 30 us -> 40 us  [the longest x18 15.5 us: matmul(): return jnp.dot(left, right, preferred_element_type=F32)]
  transfers between devices with their start and end apart: 10 -> 1, of which waited for: 6 -> 0; matrix products, arithmetic and copies ran while one was open for 7% -> 7% of each run, Pallas kernels for 0% -> 0%
where the time goes in v1:
time: 172 us
  Pallas kernels  92.6 us (54%)
  matrix products  40 us (23%)
  local copies, waits for them, and re-layouts  18 us (10%)
  other arithmetic  17.3 us (10%)
  starting transfers between devices  2.14 us (1%)
  between operations  1.73 us (1%)
    pallas_call x1, Pallas kernels, reduce(): pl.pallas_call(partial(reduce_kernel, n, c), out_shape=[shape(w.shape[1:]...  49.2 us
    pallas_call x1, Pallas kernels, gather(): pl.pallas_call(partial(gather_kernel, n, c), out_shape=[shape((n, *w.shap...  43.4 us
    dot_general x18, matrix products, matmul(): return jnp.dot(left, right, preferred_element_type=F32)  15.5 us
    dot_general x17, matrix products, matmul_tn(): lax.dot_general(left, right, (((0,), (0,)), ((), ())), preferred_element_...  12.5 us
    dot_general x17, matrix products, matmul_nt(): lax.dot_general(left, right, (((1,), (1,)), ((), ())), preferred_element_...  9.95 us
    unnamed x159, local copies, waits for them, and re-layouts  4.78 us
    slice x3, local copies, waits for them, and re-layouts, per_device(): parts.append(flat[start:start + piece.shape[0]])  3.77 us
  transfers between devices with their start and end apart: 1, of which 0 were waited for; matrix products, arithmetic and copies ran while one was open for 7% of the time, Pallas kernels for 0%

profile of v1, /device:TPU:0, one launch (start us, length us, event | category | flops | bytes accessed | tf_op | source)
XLA Modules:
  0.0 171.7 jit_solution(7015820444031146100)
XLA Ops:
  1.4 1.3 convert_reduce_fusion.1
  2.9 1.3 fusion.155
  5.1 43.4 %gather.1 = (bf16[16,24,1152]{2,1,0:T(8,128)(2,1)}, bf16[16,24,384]{2,1,0:T(8,128)(2,1)}, bf16[16,24,1536]{2,1,0:T(8,128)(2,1)}, bf16[16,96,384]{2,1,0:T(8,128)(...) custom-call(bf16[24,1152]{1,0:T(8,128)(2,1)} %qkv.1, ...), custom_call_target="tpu_custom_call" | custom-call | tf_op jit(solution)/shard_map/gather/pallas_call | solution.py:192
  49.5 1.1 convert_reduce_fusion
  50.9 1.3 slice_reduce_fusion.9
  53.0 1.1 subtract_multiply_fusion
  61.7 1.4 fusion.6
  68.7 1.1 fusion.158
  71.7 2.0 %convolution_add_fusion = f32[256,1536]{1,0:T(8,128)S(1)} fusion(bf16[384,1536]{1,0:T(8,128)(2,1)} %bitcast.89, f32[1536]{0:T(1024)S(1)} %add.180, f32[256,384]{1,0:T(8,128)S(1)} %get-tuple-element.73, f32[384]{0:T(512)} %get-tuple-element.64, f32[384]{0:T(512)} %get-tuple-element.65, f32[256]{0:T(256)} %add_rsqrt_fusion.1, f32[256]{0:T(256)} %copy-done.50), kind=kOutput, calls=%fused_computation.2 | convolution fusion | flops 302874624 | bytes 3156992 | tf_op jit(solution)/shard_map/dot_general | solution.py:37
  73.8 2.0 %fusion.166 = (f32[1536]{0:T(1024)}, bf16[256,1536]{1,0:T(8,128)(2,1)S(1)}) fusion(f32[256,1536]{1,0:T(8,128)S(1)} %convolution_add_fusion, bf16[1536,384]{1,0:T(8,128)(2,1)S(1)} %bitcast.102, bf16[1,256,384]{2,1,0:T(8,128)(2,1)S(1)} %copy-done.70, f32[384]{0:T(512)S(1)} %copy-done.67), kind=kOutput, calls=%fused_computation.300 | convolution fusion | flops 310540800 | bytes 3743232 | tf_op jit(solution)/shard_map/dot_general | solution.py:41
  75.8 2.0 %multiply_reduce_fusion.1 = (f32[384]{0:T(512)}, f32[256]{0:T(256)}, f32[256]{0:T(256)}, f32[384]{0:T(512)}, f32[256,384]{1,0:T(8,128)}) fusion(f32[256,384]{1,0:T(8,128)S(1)} %get-tuple-element.73, f32[256]{0:T(256)S(1)} %copy-done.55, f32[256]{0:T(256)S(1)} %copy-done.51, f32[384]{0:T(512)S(1)} %copy-done.48, bf16[384,1536]{1,0:T(8,128)(2,1)S(1)} %bitcast.90, ...), kind=kOutput, calls=%fused_computation.116 | convolution fusion | flops 302873344 | bytes 2761216 | tf_op jit(solution)/shard_map/dot_general | solution.py:41
  79.2 4.2 %fusion.51 = (f32[384]{0:T(512)}, f32[384]{0:T(512)}, bf16[1,256,384]{2,1,0:T(8,128)(2,1)}, f32[384]{0:T(512)}, f32[384]{0:T(512)}, /*index=5*/f32[256,384]{1,0:T(8,128)S(1)}) fusion(bf16[1,256,384]{2,1,0:T(8,128)(2,1)} %param.25, f32[384]{0:T(512)} %get-tuple-element.63, f32[256,384]{1,0:T(8,128)S(1)} %get-tuple-element.73, ...), kind=kOutput, calls=%fused_computation.111 | convolution fusion | flops 307591680 | bytes 4734976 | tf_op jit(solution)/shard_map/dot_general | solution.py:37
  93.5 2.1 %collective-permute-start = (bf16[256,384]{1,0:T(8,128)(2,1)}, bf16[256,384]{1,0:T(8,128)(2,1)}, u32[]{:S(2)}, u32[]{:S(2)}) collective-permute-start(bf16[256,384]{1,0:T(8,128)(2,1)} %slice.406), channel_id=1, source_target_pairs={{0,1},{1,0},{2,3},{3,2},{4,5},{5,4},{6,7},{7,6},{8,9},{9,8},{10,11... | collective-permute-start | bytes 589832 | tf_op jit(solution)/shard_map/ppermute | solution.py:501
  95.9 1.7 convolution_convert_fusion.1
  100.3 1.9 %convolution_convert_fusion = bf16[1536,384]{1,0:T(8,128)(2,1)} fusion(bf16[1,256,384]{2,1,0:T(8,128)(2,1)S(1)} %copy-done.71, f32[384]{0:T(512)S(1)} %copy-done.68, f32[256,1536]{1,0:T(8,128)S(1)} %copy-done.14), kind=kOutput, calls=%fused_computation | convolution fusion | flops 306413568 | bytes 2950656 | tf_op jit(solution)/shard_map/dot_general | solution.py:45
  102.3 1.1 pad_convert_fusion.ada
  105.1 1.0 slice_reduce_fusion
  108.2 1.5 multiply_reduce_fusion.3
  110.4 49.2 %reduce.42 = (f32[24,1152]{1,0:T(8,128)}, f32[24,384]{1,0:T(8,128)}, f32[24,1536]{1,0:T(8,128)}, f32[96,384]{1,0:T(8,128)}, f32[8,128]{1,0:T(8,128)}, /*index=5*/f32[16,1,2304]{2,1,0:T(1,128)}, f32[16,1,128]{2,1,0:T(1,128)}) custom-call(bf16[16,24,1152]{2,1,0:T(8,128)(2,1)} %pad_maximum_fusion.qkv, bf16[16,24,384]{2,1,0:T(8,128)(2,1)} %bitcast.94, ...), custom_call_target="tpu_custom_call" | custom-call | tf_op jit(solution)/shard_map/reduce/pallas_call | solution.py:365
  159.7 1.3 fusion.159
  161.0 1.2 slice.225
  162.2 1.3 slice.227
  163.4 1.4 dynamic-slice_reduce_fusion
  164.9 2.0 %fusion.74 = f32[24,2304]{1,0:T(8,128)} fusion(f32[16,24]{1,0:T(8,128)S(1)} %slice_reduce_fusion, f32[16,1,2304]{2,1,0:T(1,128)} %get-tuple-element.37), kind=kOutput, calls=%fused_computation.148 | convolution fusion | flops 10616832 | bytes 370176 | tf_op jit(solution)/shard_map/dot_general | solution.py:530
  (258 shorter events, 42.0 us)
Async XLA Ops:
  0.6 50.0 %copy-start = (bf16[1,256,384]{2,1,0:T(8,128)(2,1)S(1)}, bf16[1,256,384]{2,1,0:T(8,128)(2,1)}, u32[]{:S(2)}) copy-start(bf16[1,256,384]{2,1,0:T(8,128)(2,1)} %param.13) | copy-start | bytes 589828
  48.5 5.7 %copy-start.15 = (bf16[16,24,1152]{2,1,0:T(8,128)(2,1)S(1)}, bf16[16,24,1152]{2,1,0:T(8,128)(2,1)}, u32[]{:S(2)}) copy-start(bf16[16,24,1152]{2,1,0:T(8,128)(2,1)} %get-tuple-element.30) | copy-start | bytes 2654212
  54.2 7.5 %copy-start.1 = (bf16[512,384]{1,0:T(8,128)(2,1)}, bf16[512,384]{1,0:T(8,128)(2,1)S(1)}, u32[]{:S(2)}) copy-start(bf16[512,384]{1,0:T(8,128)(2,1)S(1)} %get-tuple-element.77) | copy-start | bytes 1179652
  63.0 4.9 %copy-start.17 = (bf16[512,384]{0,1:T(8,128)(2,1)}, bf16[512,384]{0,1:T(8,128)(2,1)S(1)}, u32[]{:S(2)}) copy-start(bf16[512,384]{0,1:T(8,128)(2,1)S(1)} %fusion.6) | copy-start | bytes 1179652
  64.6 4.1 %copy-start.21 = (bf16[16,24,384]{2,1,0:T(8,128)(2,1)S(1)}, bf16[16,24,384]{2,1,0:T(8,128)(2,1)}, u32[]{:S(2)}) copy-start(bf16[16,24,384]{2,1,0:T(8,128)(2,1)} %get-tuple-element.32) | copy-start | bytes 884740
  64.6 4.1 %copy-start.57 = (f32[384]{0:T(512)S(1)}, f32[384]{0:T(512)}, u32[]{:S(2)}) copy-start(f32[384]{0:T(512)} %add.170) | copy-start | bytes 4612
  79.2 4.3 %copy-start.22 = (bf16[16,24,384]{2,1,0:T(8,128)(2,1)S(1)}, bf16[16,24,384]{2,1,0:T(8,128)(2,1)}, u32[]{:S(2)}) copy-start(bf16[16,24,384]{2,1,0:T(8,128)(2,1)} %get-tuple-element.32) | copy-start | bytes 884740
  79.2 4.6 %copy-start.36 = (bf16[256,64]{0,1:T(8,128)(2,1)S(1)}, bf16[256,64]{0,1:T(8,128)(2,1)}, u32[]{:S(2)}) copy-start(bf16[256,64]{0,1:T(8,128)(2,1)} %get-tuple-element.87) | copy-start | bytes 98308
  79.2 4.6 %copy-start.37 = (bf16[256,64]{0,1:T(8,128)(2,1)S(1)}, bf16[256,64]{0,1:T(8,128)(2,1)}, u32[]{:S(2)}) copy-start(bf16[256,64]{0,1:T(8,128)(2,1)} %get-tuple-element.91) | copy-start | bytes 98308
  79.2 4.6 %copy-start.38 = (bf16[256,64]{0,1:T(8,128)(2,1)S(1)}, bf16[256,64]{0,1:T(8,128)(2,1)}, u32[]{:S(2)}) copy-start(bf16[256,64]{0,1:T(8,128)(2,1)} %get-tuple-element.95) | copy-start | bytes 98308
  79.2 4.6 %copy-start.39 = (bf16[256,64]{0,1:T(8,128)(2,1)S(1)}, bf16[256,64]{0,1:T(8,128)(2,1)}, u32[]{:S(2)}) copy-start(bf16[256,64]{0,1:T(8,128)(2,1)} %get-tuple-element.99) | copy-start | bytes 98308
  79.2 4.6 %copy-start.40 = (bf16[256,64]{0,1:T(8,128)(2,1)S(1)}, bf16[256,64]{0,1:T(8,128)(2,1)}, u32[]{:S(2)}) copy-start(bf16[256,64]{0,1:T(8,128)(2,1)} %get-tuple-element.103) | copy-start | bytes 98308
  79.2 4.6 %copy-start.41 = (bf16[256,64]{0,1:T(8,128)(2,1)S(1)}, bf16[256,64]{0,1:T(8,128)(2,1)}, u32[]{:S(2)}) copy-start(bf16[256,64]{0,1:T(8,128)(2,1)} %get-tuple-element.107) | copy-start | bytes 98308
  79.2 4.7 %copy-start.18 = (bf16[512,384]{0,1:T(8,128)(2,1)S(1)}, bf16[512,384]{0,1:T(8,128)(2,1)}, u32[]{:S(2)}) copy-start(bf16[512,384]{0,1:T(8,128)(2,1)} %copy-done.17) | copy-start | bytes 1179652
  91.1 4.5 %copy-start.6 = (bf16[512,384]{0,1:T(8,128)(2,1)S(1)}, bf16[512,384]{0,1:T(8,128)(2,1)}, u32[]{:S(2)}) copy-start(bf16[512,384]{0,1:T(8,128)(2,1)} %copy-done.5) | copy-start | bytes 1179652
  93.5 14.7 %collective-permute-start = (bf16[256,384]{1,0:T(8,128)(2,1)}, bf16[256,384]{1,0:T(8,128)(2,1)}, u32[]{:S(2)}, u32[]{:S(2)}) collective-permute-start(bf16[256,384]{1,0:T(8,128)(2,1)} %slice.406), channel_id=1, source_target_pairs={{0,1},{1,0},{2,3},{3,2},{4,5},{5,4},{6,7},{7,6},{8,9},{9,8},{10,11... | collective-permute-start | bytes 589832 | tf_op jit(solution)/shard_map/ppermute | solution.py:501
  104.0 4.2 %copy-start.11 = (f32[512,384]{1,0:T(8,128)S(1)}, f32[512,384]{1,0:T(8,128)}, u32[]{:S(2)}) copy-start(f32[512,384]{1,0:T(8,128)} %get-tuple-element.76) | copy-start | bytes 2359300
  110.4 57.3 %copy-start.59 = (bf16[1,384]{1,0:T(2,128)(2,1)S(1)}, bf16[1,384]{1,0:T(2,128)(2,1)}, u32[]{:S(2)}) copy-start(bf16[1,384]{1,0:T(2,128)(2,1)} %param.14) | copy-start | bytes 2308
  110.4 57.3 %copy-start.60 = (f32[1,384]{1,0:T(1,128)S(1)}, f32[1,384]{1,0:T(1,128)}, u32[]{:S(2)}) copy-start(f32[1,384]{1,0:T(1,128)} %get-tuple-element.75) | copy-start | bytes 4612
  110.4 57.8 %slice-start = ((f32[512]{0:T(512)}), f32[256]{0:T(256)S(1)}, s32[]{:S(2)}) async-start(f32[512]{0:T(512)} %copy-done.53), calls=%async_computation | async-start | bytes 2048 | tf_op jit(solution)/shard_map/slice | solution.py:433
  159.6 9.5 %copy-start.42 = (f32[24,1152]{1,0:T(8,128)S(1)}, f32[24,1152]{1,0:T(8,128)}, u32[]{:S(2)}) copy-start(f32[24,1152]{1,0:T(8,128)} %get-tuple-element.147) | copy-start | bytes 331780
  159.6 10.1 %copy-start.44 = (f32[24,384]{1,0:T(8,128)S(1)}, f32[24,384]{1,0:T(8,128)}, u32[]{:S(2)}) copy-start(f32[24,384]{1,0:T(8,128)} %get-tuple-element.149) | copy-start | bytes 110596
  159.7 10.7 %copy-start.35 = (f32[24,1536]{1,0:T(8,128)S(1)}, f32[24,1536]{1,0:T(8,128)}, u32[]{:S(2)}) copy-start(f32[24,1536]{1,0:T(8,128)} %get-tuple-element.151) | copy-start | bytes 442372
  159.7 11.4 %copy-start.34 = (f32[96,384]{1,0:T(8,128)S(1)}, f32[96,384]{1,0:T(8,128)}, u32[]{:S(2)}) copy-start(f32[96,384]{1,0:T(8,128)} %get-tuple-element.153) | copy-start | bytes 442372
  (50 other events, 110.6 us)

commit v2 on v1

v2 whole, which is shorter than its diff:
```python
from functools import partial

import jax
import jax.numpy as jnp
from jax import lax
from jax.experimental import pallas as pl
from jax.experimental.pallas import tpu as pltpu
from jax.sharding import PartitionSpec as P

HEADS = 6
HEAD = 64
MESH = pl.DeviceIdType.MESH
F32 = jnp.float32
BF16 = jnp.bfloat16


epsilon = 1e-06


def layer_stats(values):
    centered = values - jnp.mean(values, axis=-1, keepdims=True)
    inverse = lax.rsqrt(jnp.mean(centered * centered, axis=-1, keepdims=True) + epsilon)
    return (centered * inverse, inverse)


def layer_back(normed, inverse, grad_normed):
    mean_grad = jnp.mean(grad_normed, axis=-1, keepdims=True)
    mean_prod = jnp.mean(grad_normed * normed, axis=-1, keepdims=True)
    return inverse * (grad_normed - mean_grad - normed * mean_prod)


def gelu_pair(hidden):
    root = (2.0 / 3.141592653589793) ** 0.5
    square = hidden * hidden
    curve = jnp.tanh(root * (hidden + 0.044715 * square * hidden))
    cdf = 0.5 * (1.0 + curve)
    slope = cdf + 0.5 * hidden * (1.0 - curve * curve) * root * (1.0 + 3 * 0.044715 * square)
    return (hidden * cdf, slope)


def matmul(left, right):
    return jnp.dot(left, right, preferred_element_type=F32)


def matmul_nt(left, right):
    return lax.dot_general(left, right, (((1,), (1,)), ((), ())), preferred_element_type=F32)


def matmul_tn(left, right):
    return lax.dot_general(left, right, (((0,), (0,)), ((), ())), preferred_element_type=F32)


def flip(index, mask):
    return index + mask - 2 * mask * ((index // mask) % 2)


def loop(count, body):
    def step(i, carry):
        body(i)
        return carry

    lax.fori_loop(0, count, step, 0)


def remote(src, dst, send, recv, **device):
    return pltpu.make_async_remote_copy(
        src_ref=src, dst_ref=dst, send_sem=send, recv_sem=recv,
        device_id=device, device_id_type=MESH,
    )


def meet(n, c, me, row):
    barrier = pltpu.get_barrier_semaphore()

    def greet_fsdp(k):
        pl.semaphore_signal(
            barrier, inc=1, device_id={"fsdp": (me + 1 + k) % n}, device_id_type=MESH
        )

    def greet_ctx(k):
        pl.semaphore_signal(
            barrier, inc=1, device_id={"ctx": (row + 1 + k) % c}, device_id_type=MESH
        )

    loop(n - 1, greet_fsdp)
    loop(c - 1, greet_ctx)
    pl.semaphore_wait(barrier, n + c - 2)


def gather_kernel(
    n, c,
    qkv, out, fc1, fc2, tok, cond, ada, ada_bias, small,
    qkv_all, out_all, fc1_all, fc2_all, tok_all, cond_out, mod, small_all,
    cond_all, part, mod_all,
    send_w, recv_w, send_t, recv_t, send_c, recv_c, send_m, recv_m, send_s, recv_s,
):
    me, row = lax.axis_index("fsdp"), lax.axis_index("ctx")
    own = (qkv, out, fc1, fc2)
    full = (qkv_all, out_all, fc1_all, fc2_all)
    stages = n.bit_length() - 1
    meet(n, c, me, row)

    def cond_copy(to, sender):
        return remote(
            cond.at[to], cond_all.at[sender], send_c.at[to], recv_c.at[sender], fsdp=to
        )

    def small_copy(to, sender):
        return remote(small, small_all.at[sender], send_s.at[to], recv_s.at[sender], fsdp=to)

    def mod_copy(to, sender):
        return remote(part.at[to], mod_all.at[sender], send_m.at[to], recv_m.at[sender], fsdp=to)

    def tok_copy(to, sender):
        return remote(tok, tok_all.at[sender], send_t.at[to], recv_t.at[sender], ctx=to)

    def weight_copy(w, s, block, mine):
        return remote(
            own[w] if mine else full[w].at[block],
            full[w].at[block],
            send_w.at[w, s, block],
            recv_w.at[w, block],
            fsdp=flip(me, n >> (s + 1)),
        )

    def others(body):
        loop(n - 1, lambda k: body((me + 1 + k) % n))

    def siblings(body):
        loop(c - 1, lambda k: body((row + 1 + k) % c))

    relay = stages - 2 if c == 2 and stages >= 3 else -1

    def relay_copy(w, block):
        return remote(
            full[w].at[block], full[w].at[block],
            send_w.at[w, stages, block], recv_w.at[w, block], ctx=(row + 1) % c,
        )

    def forward(w, s, block, mine):
        if s != relay:
            weight_copy(w, s, block, mine).start()
            return

        @pl.when((block // (2 * (n >> (s + 1)))) % 2 == row)
        def _():
            weight_copy(w, s, block, mine).start()

    others(lambda to: cond_copy(to, me).start())
    for w in range(4):
        for s in range(stages):
            forward(w, s, me, True)
    others(lambda to: small_copy(to, me).start())
    siblings(lambda to: tok_copy(to, row).start())
    for w in range(4):
        full[w][me] = own[w][...]
    tok_all[row] = tok[...]
    small_all[me] = small[...]
    cond_all[me] = cond[me]
    others(lambda peer: cond_copy(peer, peer).wait_recv())
    lane = lax.broadcasted_iota(jnp.int32, cond_all.shape[1:], 1)
    columns = jnp.zeros(cond_all.shape[1:], F32)
    for i in range(n):
        columns = jnp.where(lane == i, cond_all[i], columns)
    cond_out[...] = columns
    partial_mod = matmul_tn(columns.astype(BF16), ada[...])
    for i in range(n):
        part[i] = partial_mod[i : i + 1, :] + ada_bias[...]
    others(lambda to: mod_copy(to, me).start())
    mod_all[me] = part[me]

    for s in range(stages):
        mask = n >> (s + 1)
        origin = flip(me, mask) % (2 * mask)

        def arrived(t, s=s, mask=mask, origin=origin, across=False):
            block = origin + t * (2 * mask)
            for w in range(4):
                weight_copy(w, s, block, False).wait_recv()
                if across:
                    relay_copy(w, block).start()
                for later in range(s + 1, stages):
                    forward(w, later, block, False)

        if s == relay:
            loop(1 << (s - 1), lambda t: arrived(2 * t + row, across=True))
            loop(1 << (s - 1), lambda t: arrived(2 * t + 1 - row))
        else:
            loop(1 << s, arrived)

    others(lambda peer: mod_copy(peer, peer).wait_recv())
    total = mod_all[0]
    for i in range(1, n):
        total = total + mod_all[i]
    mod[...] = total
    others(lambda peer: small_copy(peer, peer).wait_recv())
    siblings(lambda peer: tok_copy(peer, peer).wait_recv())
    for s in range(stages):
        mask = n >> (s + 1)

        def left(t, s=s, mask=mask):
            block = me % (2 * mask) + t * (2 * mask)
            for w in range(4):
                weight_copy(w, s, block, False).wait_send()

        def crossed(t, mask=mask):
            block = flip(me, mask) % (2 * mask) + t * (2 * mask)
            for w in range(4):
                relay_copy(w, block).wait_send()

        if s == relay:
            loop(1 << (s - 1), lambda t: left(2 * t + row))
            loop(1 << (s - 1), lambda t: crossed(2 * t + row))
        else:
            loop(1 << s, left)
    others(lambda to: cond_copy(to, me).wait_send())
    others(lambda to: small_copy(to, me).wait_send())
    others(lambda to: mod_copy(to, me).wait_send())
    siblings(lambda to: tok_copy(to, row).wait_send())


def vmem(count):
    return [pl.BlockSpec(memory_space=pltpu.VMEM)] * count


def gather(n, c, qkv, out, fc1, fc2, tok, cond, ada, ada_bias, small):
    stages = n.bit_length() - 1
    shape = jax.ShapeDtypeStruct
    dma = pltpu.SemaphoreType.DMA
    return pl.pallas_call(
        partial(gather_kernel, n, c),
        out_shape=[shape((n, *w.shape), BF16) for w in (qkv, out, fc1, fc2)]
        + [
            shape((c, *tok.shape), BF16),
            shape(cond.shape[1:], F32),
            shape(ada_bias.shape, F32),
            shape((n, *small.shape), F32),
        ],
        in_specs=vmem(9),
        out_specs=vmem(8),
        scratch_shapes=[
            pltpu.VMEM(cond.shape, F32),
            pltpu.VMEM((n, *ada_bias.shape), F32),
            pltpu.VMEM((n, *ada_bias.shape), F32),
            dma((4, stages + 1, n)), dma((4, n)),
            dma((c,)), dma((c,)), dma((n,)), dma((n,)), dma((n,)), dma((n,)), dma((n,)), dma((n,)),
        ],
        compiler_params=pltpu.CompilerParams(collective_id=0, has_side_effects=True),
        name="gather",
    )(qkv, out, fc1, fc2, tok, cond, ada, ada_bias, small)


def reduce_kernel(
    n, c,
    qkv, out, fc1, fc2, line, ada, columns, tok, mod, after, hid_own, hid_sent,
    qkv_sum, out_sum, fc1_sum, fc2_sum, grad_input, grad_ada, total_line, back_all,
    *scratch,
):
    stages = n.bit_length() - 1
    me, row = lax.axis_index("fsdp"), lax.axis_index("ctx")
    given = (qkv, out, fc1, fc2)
    sums = (qkv_sum, out_sum, fc1_sum, fc2_sum)
    arrays = len(given)
    incoming = [scratch[w * stages : (w + 1) * stages] for w in range(arrays)]
    scratch = scratch[arrays * stages :]
    kept = [scratch[w * stages : (w + 1) * stages] for w in range(arrays)]
    scratch = scratch[arrays * stages :]
    shares, scratch = scratch[:arrays], scratch[arrays:]
    (gm, gm_ctx, gm_mine, gm_all, back, hid, send_r, recv_r, send_x, recv_x, send_g, recv_g,
     send_f, recv_f, send_b, recv_b, send_h, recv_h) = scratch
    width = tok.shape[1]
    meet(n, c, me, row)

    def others(body):
        loop(n - 1, lambda k: body((me + 1 + k) % n))

    def siblings(body):
        loop(c - 1, lambda k: body((row + 1 + k) % c))

    def ctx_gm(to, sender):
        return remote(gm, gm_ctx.at[sender], send_g.at[to], recv_g.at[sender], ctx=to)

    def fsdp_gm(to, sender):
        return remote(gm_mine, gm_all.at[sender], send_f.at[to], recv_f.at[sender], fsdp=to)

    def back_copy(to, sender):
        return remote(back.at[to], back_all.at[sender], send_b.at[to], recv_b.at[sender], fsdp=to)

    def share_copy(w, to, sender):
        return remote(
            shares[w].at[row], shares[w].at[sender], send_x.at[w, to], recv_x.at[w, sender], ctx=to
        )

    def bit(s):
        return (me // (1 << s)) % 2

    def source(w, s):
        return given[w] if s == 0 else kept[w][s - 1]

    def halve(w, s, j):
        return remote(
            source(w, s).at[2 * j + 1 - bit(s)],
            incoming[w][s].at[j],
            send_r.at[w, s, j],
            recv_r.at[w, s, j],
            fsdp=flip(me, 1 << s),
        )

    def hid_copy(k):
        return remote(
            hid_sent.at[k], hid.at[k], send_h.at[k], recv_h.at[k], ctx=(row + 1 + k) % c
        )

    for k in range(c - 1):
        hid_copy(k).start()

    def send_all(s, base, step, count):
        def body(t):
            for w in range(arrays):
                halve(w, s, base + step * t).start()

        loop(count, body)

    send_all(0, 1 - bit(1), 2, n // 4)
    send_all(0, bit(1), 2, n // 4)

    normed, inverse = layer_stats(tok[...].astype(F32))
    grad_hidden = hid_own[...]
    for k in range(c - 1):
        hid_copy(k).wait_recv()
        grad_hidden = grad_hidden + hid[k].astype(F32)
    grad_input[...] = (
        after[...]
        + layer_back(normed, inverse, grad_hidden * (1.0 + mod[:, width : 2 * width]))
    ).astype(BF16)
    gm[:, :width] = jnp.sum(grad_hidden, axis=0, keepdims=True)
    gm[:, width : 2 * width] = jnp.sum(grad_hidden * normed, axis=0, keepdims=True)
    gm[:, 2 * width :] = line[:, 2 * width :]
    siblings(lambda to: ctx_gm(to, row).start())
    gm_ctx[row] = gm[...]
    siblings(lambda peer: ctx_gm(peer, peer).wait_recv())
    total = gm_ctx[0]
    for i in range(1, c):
        total = total + gm_ctx[i]
    gm_mine[...] = total
    gm_all[me] = total
    others(lambda to: fsdp_gm(to, me).start())

    def backward():
        others(lambda peer: fsdp_gm(peer, peer).wait_recv())
        rows = lax.broadcasted_iota(jnp.int32, (n, gm.shape[1]), 0)
        stacked = jnp.zeros((n, gm.shape[1]), F32)
        for i in range(n):
            stacked = jnp.where(rows == i, jnp.broadcast_to(gm_all[i], stacked.shape), stacked)
        wide = 6 * width
        total_line[...] = jnp.sum(stacked, axis=0, keepdims=True)
        grad_ada[...] = lax.dot_general(
            columns[...][:, :n], stacked[:, :wide], (((1,), (0,)), ((), ())),
            preferred_element_type=F32, precision=lax.Precision.HIGHEST,
        )
        product = lax.dot_general(
            stacked[:, :wide], ada[...], (((1,), (1,)), ((), ())),
            preferred_element_type=F32, precision=lax.Precision.HIGHEST,
        )
        for i in range(n):
            back[i] = product[i : i + 1, :]
        others(lambda to: back_copy(to, me).start())
        back_all[me] = back[me]

    def add(w, s, j):
        halve(w, s, j).wait_recv()
        value = source(w, s)[2 * j + bit(s)].astype(F32) + incoming[w][s][j].astype(F32)
        if s == stages - 1:
            shares[w][row] = value.astype(given[w].dtype)
        else:
            kept[w][s][j] = value.astype(given[w].dtype)

    for s in range(stages):
        if s == stages - 1:
            for w in range(arrays):
                add(w, s, 0)
                siblings(lambda to, w=w: share_copy(w, to, row).start())
            continue

        def first(t, s=s):
            j = 2 * t + 1 - bit(s + 1)
            for w in range(arrays):
                add(w, s, j)
                halve(w, s + 1, t).start()

        def second(t, s=s):
            for w in range(arrays):
                add(w, s, 2 * t + bit(s + 1))

        loop(n >> (s + 2), first)
        loop(n >> (s + 2), second)
        if s == 0:
            backward()

    for w in range(arrays):
        siblings(lambda peer, w=w: share_copy(w, peer, peer).wait_recv())
        value = shares[w][0].astype(F32)
        for i in range(1, c):
            value = value + shares[w][i].astype(F32)
        sums[w][...] = value
    others(lambda peer: back_copy(peer, peer).wait_recv())

    for k in range(c - 1):
        hid_copy(k).wait_send()
    siblings(lambda to: ctx_gm(to, row).wait_send())
    others(lambda to: fsdp_gm(to, me).wait_send())
    others(lambda to: back_copy(to, me).wait_send())
    for s in range(stages):

        def sent(j, s=s):
            for w in range(arrays):
                halve(w, s, j).wait_send()

        loop(n >> (s + 1), sent)
    for w in range(arrays):
        siblings(lambda to, w=w: share_copy(w, to, row).wait_send())


def reduce(n, c, qkv, out, fc1, fc2, line, ada, columns, tok, mod, after, hid_own, hid_sent):
    stages = n.bit_length() - 1
    shape = jax.ShapeDtypeStruct
    dma = pltpu.SemaphoreType.DMA
    given = (qkv, out, fc1, fc2)
    halves = [
        pltpu.VMEM((n >> (s + 1), *w.shape[1:]), w.dtype) for w in given for s in range(stages)
    ]
    back = (n, 1, ada.shape[0])
    return pl.pallas_call(
        partial(reduce_kernel, n, c),
        out_shape=[shape(w.shape[1:], F32) for w in given]
        + [
            shape(tok.shape, BF16),
            shape((columns.shape[0], mod.shape[1]), F32),
            shape(line.shape, F32),
            shape(back, F32),
        ],
        in_specs=vmem(12),
        out_specs=vmem(8),
        scratch_shapes=halves
        + halves
        + [pltpu.VMEM((c, *w.shape[1:]), w.dtype) for w in given]
        + [
            pltpu.VMEM(line.shape, F32),
            pltpu.VMEM((c, *line.shape), F32),
            pltpu.VMEM(line.shape, F32),
            pltpu.VMEM((n, *line.shape), F32),
            pltpu.VMEM(back, F32),
            pltpu.VMEM(hid_sent.shape, BF16),
            dma((4, stages, n // 2)), dma((4, stages, n // 2)),
            dma((4, c)), dma((4, c)), dma((c,)), dma((c,)),
            dma((n,)), dma((n,)), dma((n,)), dma((n,)), dma((c,)), dma((c,)),
        ],
        compiler_params=pltpu.CompilerParams(collective_id=1, has_side_effects=True),
        name="reduce",
    )(qkv, out, fc1, fc2, line, ada, columns, tok, mod, after, hid_own, hid_sent)


def head(array, h):
    return array[:, h * HEAD : (h + 1) * HEAD]


def block_kernel(
    c,
    qkv_ref, out_ref, fc1_ref, fc2_ref, tok_ref, mod_ref, bias_ref, cot_ref,
    result_ref, after_ref, hid_own_ref, hid_sent_ref, qkv_grad, out_grad, fc1_grad, fc2_grad,
    line_ref,
):
    width = cot_ref.shape[1]
    rows = cot_ref.shape[0]
    hidden_width = fc1_ref.shape[1]
    scale_factor = HEAD ** (-0.5)
    shift_one, scale_one, gate_one, shift_two, scale_two, gate_two = (
        mod_ref[:, k * width : (k + 1) * width] for k in range(6)
    )
    starts = (0, width, 2 * width, 3 * width, 3 * width + hidden_width, 4 * width + hidden_width)
    query_bias, value_bias, out_bias, fc1_bias, fc2_bias = (
        bias_ref[:, a:b] for a, b in zip(starts, starts[1:])
    )
    residual_all = tok_ref[...].astype(F32)
    normed_all, _ = layer_stats(residual_all)
    hidden_all = (normed_all * (1.0 + scale_one) + shift_one).astype(BF16)
    residual, hidden_one = residual_all[:rows], hidden_all[:rows]
    queries = (matmul(hidden_one, qkv_ref[:, :width]) + query_bias).astype(BF16)
    keys = matmul(hidden_all, qkv_ref[:, width : 2 * width]).astype(BF16)
    values = (matmul(hidden_all, qkv_ref[:, 2 * width :]) + value_bias).astype(BF16)
    probabilities, mixed_heads = [], []
    for h in range(HEADS):
        scores = matmul_nt(head(queries, h), head(keys, h)) * scale_factor
        raised = jnp.exp(scores - jnp.max(scores, axis=1, keepdims=True))
        probability = raised * (1.0 / jnp.sum(raised, axis=1, keepdims=True))
        probabilities.append(probability)
        mixed_heads.append(matmul(probability.astype(BF16), head(values, h)))
    mixed = jnp.concatenate(mixed_heads, axis=1).astype(BF16)
    attn_out = matmul(mixed, out_ref[...]) + out_bias
    after_attn = residual + gate_one * attn_out
    normed_two, inverse_two = layer_stats(after_attn)
    hidden_two = (normed_two * (1.0 + scale_two) + shift_two).astype(BF16)
    pre_act = matmul(hidden_two, fc1_ref[...]) + fc1_bias
    activated, slope = gelu_pair(pre_act)
    activated = activated.astype(BF16)
    mlp_out = matmul(activated, fc2_ref[...]) + fc2_bias
    result_ref[...] = (after_attn + gate_two * mlp_out).astype(BF16)

    def total(array):
        return jnp.sum(array, axis=0, keepdims=True)

    grad_result = cot_ref[...].astype(F32)
    grad_mlp_float = grad_result * gate_two
    grad_mlp = grad_mlp_float.astype(BF16)
    fc2_grad[...] = matmul_tn(activated, grad_mlp).astype(BF16)
    grad_pre = slope * matmul_nt(grad_mlp, fc2_ref[...])
    grad_pre_half = grad_pre.astype(BF16)
    fc1_grad[...] = matmul_tn(hidden_two, grad_pre_half).astype(BF16)
    grad_hidden_two = matmul_nt(grad_pre_half, fc1_ref[...])
    grad_after = grad_result + layer_back(
        normed_two, inverse_two, grad_hidden_two * (1.0 + scale_two)
    )
    after_ref[...] = grad_after
    grad_attn_float = grad_after * gate_one
    grad_attn = grad_attn_float.astype(BF16)
    out_grad[...] = matmul_tn(mixed, grad_attn).astype(BF16)
    grad_mixed = matmul_nt(grad_attn, out_ref[...]).astype(BF16)
    grad_q, grad_k, grad_v = [], [], []
    for h in range(HEADS):
        grad_head = head(grad_mixed, h)
        inner = jnp.sum(
            grad_head.astype(F32) * head(mixed, h).astype(F32), axis=1, keepdims=True
        )
        grad_prob = matmul_nt(grad_head, head(values, h))
        grad_scores = (probabilities[h] * (grad_prob - inner) * scale_factor).astype(BF16)
        grad_q.append(matmul(grad_scores, head(keys, h)))
        grad_k.append(matmul_tn(grad_scores, head(queries, h)))
        grad_v.append(matmul_tn(probabilities[h].astype(BF16), grad_head))
    grad_query = jnp.concatenate(grad_q, axis=1)
    grad_value = jnp.concatenate(grad_v, axis=1)
    grad_kv = jnp.concatenate(grad_k + grad_v, axis=1).astype(BF16)
    query_half = grad_query.astype(BF16)
    hid_kv = matmul_nt(grad_kv, qkv_ref[:, width:])
    hid_own_ref[...] = hid_kv[:rows] + matmul_nt(query_half, qkv_ref[:, :width])
    for k in range(1, c):
        hid_sent_ref[k - 1] = hid_kv[k * rows : (k + 1) * rows].astype(BF16)
    qkv_grad[:, :width] = matmul_tn(hidden_one, query_half).astype(BF16)
    qkv_grad[:, width:] = matmul_tn(hidden_all, grad_kv).astype(BF16)
    line = (
        jnp.zeros((1, 2 * width), F32),
        total(grad_after * attn_out),
        total(grad_hidden_two),
        total(grad_hidden_two * normed_two),
        total(grad_result * mlp_out),
        total(grad_query),
        total(grad_value),
        total(grad_attn_float),
        total(grad_pre),
        total(grad_mlp_float),
    )
    start = 0
    for piece in line:
        line_ref[:, start : start + piece.shape[1]] = piece
        start += piece.shape[1]


def block(c, qkv, out, fc1, fc2, tok, mod, bias, cot):
    shape = jax.ShapeDtypeStruct
    return pl.pallas_call(
        partial(block_kernel, c),
        out_shape=[
            shape(cot.shape, BF16),
            shape(cot.shape, F32),
            shape(cot.shape, F32),
            shape((c - 1, *cot.shape), BF16),
            shape(qkv.shape, BF16),
            shape(out.shape, BF16),
            shape(fc1.shape, BF16),
            shape(fc2.shape, BF16),
            shape((1, mod.shape[1] + bias.shape[1]), F32),
        ],
        in_specs=vmem(8),
        out_specs=vmem(9),
        name="block",
    )(qkv, out, fc1, fc2, tok, mod, bias, cot)


def per_device(
    n, c,
    tokens, condition,
    ada_weight, ada_bias, qkv_weight, qv_bias, out_weight, out_bias,
    fc1_weight, fc1_bias, fc2_weight, fc2_bias,
    cotangent,
):
    latents, local_rows, width = tokens.shape
    me, row = lax.axis_index("fsdp"), lax.axis_index("ctx")
    scale_factor = HEAD ** (-0.5)
    tok = tokens[0]
    slice_rows = ada_weight.shape[0]
    cond_float = condition.astype(F32)
    cond_silu = jax.nn.silu(cond_float).astype(BF16)
    cond_columns = jnp.broadcast_to(
        cond_silu.astype(F32).reshape(n, slice_rows, 1), (n, slice_rows, 128)
    )
    bias_row = lax.dynamic_update_slice(
        jnp.zeros((1, ada_bias.shape[0] * n), F32),
        ada_bias.astype(F32)[None, :],
        (0, me * ada_bias.shape[0]),
    )
    biases = jnp.concatenate([qv_bias, out_bias, fc1_bias, fc2_bias]).astype(F32)
    small = jnp.pad(biases, (0, 256 - biases.shape[0]))[None, :]
    qkv_all, out_all, fc1_all, fc2_all, tok_all, columns, modulation, small_all = gather(
        n, c, qkv_weight, out_weight, fc1_weight, fc2_weight, tok, cond_columns,
        ada_weight, bias_row, small,
    )
    pieces, start = [], 0
    for piece in (qv_bias, out_bias, fc1_bias, fc2_bias):
        pieces.append(small_all[:, 0, start : start + piece.shape[0]].reshape(1, -1))
        start += piece.shape[0]
    order = [lax.rem(row + k, c) for k in range(c)]
    rotated = jnp.concatenate([tok] + [tok_all[i] for i in order[1:]], axis=0)
    result, after, hid_own, hid_sent, grad_qkv, grad_out, grad_fc1, grad_fc2, line = block(
        c,
        qkv_all.reshape(-1, qkv_weight.shape[1]),
        out_all.reshape(-1, width),
        fc1_all.reshape(-1, fc1_weight.shape[1]),
        fc2_all.reshape(-1, width),
        rotated, modulation, jnp.concatenate(pieces, axis=1), cotangent[0],
    )
    ada_rows = jnp.pad(ada_weight.astype(F32), ((0, 128 - slice_rows), (0, 0)))
    qkv_sum, out_sum, fc1_sum, fc2_sum, grad_input, grad_ada_w, total_line, back_all = reduce(
        n, c,
        grad_qkv.reshape(qkv_all.shape),
        grad_out.reshape(out_all.shape),
        grad_fc1.reshape(fc1_all.shape),
        grad_fc2.reshape(fc2_all.shape),
        line, ada_rows, columns, tok, modulation, after, hid_own, hid_sent,
    )
    ada_back_term = back_all[:, 0, :slice_rows].reshape(1, -1)
    grad_cond = jax.vjp(jax.nn.silu, cond_float)[1](ada_back_term)[0]
    parts, start = [], 0
    for piece in (ada_bias, qv_bias, out_bias, fc1_bias, fc2_bias):
        size = piece.shape[0]
        parts.append(lax.dynamic_slice(total_line, (0, start + me * size), (1, size))[0])
        start += n * size
    return (
        result[None], grad_input[None], grad_cond,
        grad_ada_w, parts[0],
        qkv_sum, parts[1], out_sum, parts[2], fc1_sum, parts[3], fc2_sum, parts[4],
    )


def solution(mesh):
    n, c = mesh.shape["fsdp"], mesh.shape["ctx"]
    return jax.shard_map(
        partial(per_device, n, c),
        mesh=mesh,
        in_specs=(
            P("fsdp", "ctx", None),
            P("fsdp", None),
            P("fsdp", None),
            P("fsdp"),
            P("fsdp", None),
            P("fsdp"),
            P("fsdp", None),
            P("fsdp"),
            P("fsdp", None),
            P("fsdp"),
            P("fsdp", None),
            P("fsdp"),
            P("fsdp", "ctx", None),
        ),
        out_specs=(
            P("fsdp", "ctx", None),
            P("fsdp", "ctx", None),
            P("fsdp", None),
            P("fsdp", None),
            P("fsdp"),
            P("fsdp", None),
            P("fsdp"),
            P("fsdp", None),
            P("fsdp"),
            P("fsdp", None),
            P("fsdp"),
            P("fsdp", None),
            P("fsdp"),
        ),
        check_vma=False,
    )
```

time: 172 us -> 143 us (0.83)
  matrix products: 40 us -> 0 us
  Pallas kernels: 92.6 us -> 119 us
  other arithmetic: 17.3 us -> 5.82 us
  starting transfers between devices: 2.14 us -> 0 us
    dot_general x53 -> x0, matrix products: 40 us -> none  [the longest x18 15.5 us: matmul(): return jnp.dot(left, right, preferred_element_type=F32)]
    pallas_call x0 -> x1, Pallas kernels: none -> 14.1 us  [block(): pl.pallas_call(partial(block_kernel, c), out_shape=[shape(cot.shape, BF16...]
    pallas_call x1, Pallas kernels: 49.2 us -> 56.2 us  [reduce(): pl.pallas_call(partial(reduce_kernel, n, c), out_shape=[shape(w.shape[1:]...]
    slice x8 -> x0, local copies, waits for them, and re-layouts: 5.55 us -> none  [the longest x3 3.77 us: per_device(): parts.append(flat[start:start + piece.shape[0]])]
    pallas_call x1, Pallas kernels: 43.4 us -> 48.5 us  [gather(): pl.pallas_call(partial(gather_kernel, n, c), out_shape=[shape((n, *w.shap...]
    reduce_sum x13 -> x0, other arithmetic: 4.63 us -> none  [the longest x1 1.42 us: per_device(): jnp.sum(lax.dynamic_slice(mod_all, (0, me * ada_bias.shape[0]), (n, ada_b...]
    squeeze x0 -> x3, local copies, waits for them, and re-layouts: none -> 3.82 us  [per_device(): lax.dynamic_slice(total_line, (0, start + me * size), (1, size))[0]]
    add x3 -> x0, local copies, waits for them, and re-layouts: 2.17 us -> none  [the longest x1 0.77 us: per_device(): pre_act = matmul(hidden_two, fc1_full) + fc1_bias_full]
  transfers between devices with their start and end apart: 1 -> 0, of which waited for: 0 -> 0; matrix products, arithmetic and copies ran while one was open for 7% -> 0% of each run, Pallas kernels for 0% -> 0%
where the time goes in v2:
time: 143 us
  Pallas kernels  119 us (83%)
  local copies, waits for them, and re-layouts  17.3 us (12%)
  other arithmetic  5.82 us (4%)
    pallas_call x1, Pallas kernels, reduce(): pl.pallas_call(partial(reduce_kernel, n, c), out_shape=[shape(w.shape[1:]...  56.2 us
    pallas_call x1, Pallas kernels, gather(): pl.pallas_call(partial(gather_kernel, n, c), out_shape=[shape((n, *w.shap...  48.5 us
    pallas_call x1, Pallas kernels, block(): pl.pallas_call(partial(block_kernel, c), out_shape=[shape(cot.shape, BF16...  14.1 us
    unnamed x20, local copies, waits for them, and re-layouts  6.78 us
    squeeze x3, local copies, waits for them, and re-layouts, per_device(): lax.dynamic_slice(total_line, (0, start + me * size), (1, size))[0]  3.82 us

profile of v2, /device:TPU:0, one launch (start us, length us, event | category | flops | bytes accessed | tf_op | source)
XLA Modules:
  0.0 142.8 jit_solution(17157891143049675544)
XLA Ops:
  0.7 0.7 broadcast_in_dim.41
  1.5 0.7 convert_reduce_fusion
  2.3 0.8 broadcast_in_dim.32.cond
  3.1 1.3 fusion.9
  4.5 48.5 %gather.1 = (bf16[16,24,1152]{2,1,0:T(8,128)(2,1)}, bf16[16,24,384]{2,1,0:T(8,128)(2,1)}, bf16[16,24,1536]{2,1,0:T(8,128)(2,1)}, bf16[16,96,384]{2,1,0:T(8,128)(...) custom-call(bf16[24,1152]{1,0:T(8,128)(2,1)} %qkv.1, ...), custom_call_target="tpu_custom_call" | custom-call | tf_op jit(solution)/shard_map/gather/pallas_call | solution.py:230
  53.0 0.8 slice_reduce_fusion.3
  54.0 0.8 slice_reduce_fusion.2
  54.9 0.7 slice_reduce_fusion.4
  56.3 0.9 dynamic-slice_bitcast_fusion
  57.3 0.8 pad_maximum_fusion.tok_ref
  58.1 14.1 %block.1 = (bf16[256,384]{1,0:T(8,128)(2,1)}, f32[256,384]{1,0:T(8,128)}, f32[256,384]{1,0:T(8,128)}, bf16[1,256,384]{2,1,0:T(8,128)(2,1)}, bf16[384,1152]{1,0:T...) custom-call(bf16[384,1152]{1,0:T(8,128)(2,1)} %bitcast.32, ...), custom_call_target="tpu_custom_call" | custom-call | tf_op jit(solution)/shard_map/block/pallas_call | solution.py:569
  72.2 1.1 pad_convert_fusion.ada
  73.3 56.2 %reduce.23 = (f32[24,1152]{1,0:T(8,128)}, f32[24,384]{1,0:T(8,128)}, f32[24,1536]{1,0:T(8,128)}, f32[96,384]{1,0:T(8,128)}, bf16[256,384]{1,0:T(8,128)(2,1)}, /*...) custom-call(bf16[16,24,1152]{2,1,0:T(8,128)(2,1)} %bitcast.33, bf16[16,24,384]{2,1,0:T(8,128)(2,1)} %bitcast.35, ...), custom_call_target="tpu_custom_call" | custom-call | tf_op jit(solution)/shard_map/reduce/pallas_call | solution.py:433
  129.5 1.3 fusion.13
  130.8 0.7 slice_reduce_fusion
  132.2 1.2 fusion.10
  133.5 1.3 fusion.12
  134.7 1.3 constant_dynamic-slice_fusion.4
  136.0 1.6 %copy.33 = bf16[1,256,384]{2,1,0:T(8,128)(2,1)} copy(bf16[1,256,384]{2,1,0:T(8,128)(2,1)} %bitcast.36) | data formatting | bytes 393216
  137.6 1.6 %copy.34 = f32[24,2304]{1,0:T(8,128)} copy(f32[24,2304]{1,0:T(8,128)} %get-tuple-element.85) | data formatting | bytes 442368
  139.3 1.5 %copy.35 = f32[24,1152]{1,0:T(8,128)} copy(f32[24,1152]{1,0:T(8,128)} %get-tuple-element.87) | data formatting | bytes 221184
  140.8 0.6 copy.36
  141.4 0.7 copy.37
  142.1 0.7 copy.38
  (24 shorter events, 1.9 us)
Async XLA Ops:
  0.6 56.6 %copy-start = (bf16[1,256,384]{2,1,0:T(8,128)(2,1)S(1)}, bf16[1,256,384]{2,1,0:T(8,128)(2,1)}, u32[]{:S(2)}) copy-start(bf16[1,256,384]{2,1,0:T(8,128)(2,1)} %param.13) | copy-start | bytes 589828
  1.5 3.0 %copy-start.5 = (f32[1,2304]{1,0:T(1,128)}, f32[1,2304]{1,0:T(1,128)S(1)}, u32[]{:S(2)}) copy-start(f32[1,2304]{1,0:T(1,128)S(1)} %dynamic_update_slice.3.ada_bias) | copy-start | bytes 27652
  58.1 14.2 %copy-start.1 = (bf16[24,2304]{1,0:T(8,128)(2,1)S(1)}, bf16[24,2304]{1,0:T(8,128)(2,1)}, u32[]{:S(2)}) copy-start(bf16[24,2304]{1,0:T(8,128)(2,1)} %ada.1) | copy-start | bytes 331780
  73.3 58.3 %copy-start.6 = (bf16[1,384]{1,0:T(2,128)(2,1)S(1)}, bf16[1,384]{1,0:T(2,128)(2,1)}, u32[]{:S(2)}) copy-start(bf16[1,384]{1,0:T(2,128)(2,1)} %param.14) | copy-start | bytes 2308
  129.5 11.3 %copy-start.4 = (f32[24,384]{1,0:T(8,128)S(1)}, f32[24,384]{1,0:T(8,128)}, u32[]{:S(2)}) copy-start(f32[24,384]{1,0:T(8,128)} %get-tuple-element.89) | copy-start | bytes 110596
  129.5 11.9 %copy-start.3 = (f32[24,1536]{1,0:T(8,128)S(1)}, f32[24,1536]{1,0:T(8,128)}, u32[]{:S(2)}) copy-start(f32[24,1536]{1,0:T(8,128)} %get-tuple-element.91) | copy-start | bytes 442372
  129.5 12.6 %copy-start.2 = (f32[96,384]{1,0:T(8,128)S(1)}, f32[96,384]{1,0:T(8,128)}, u32[]{:S(2)}) copy-start(f32[96,384]{1,0:T(8,128)} %get-tuple-element.93) | copy-start | bytes 442372

commit v3 on v2

--- a/solution.py
+++ b/solution.py
@@ -129,27 +129,10 @@
     def siblings(body):
         loop(c - 1, lambda k: body((row + 1 + k) % c))
 
-    relay = stages - 2 if c == 2 and stages >= 3 else -1
-
-    def relay_copy(w, block):
-        return remote(
-            full[w].at[block], full[w].at[block],
-            send_w.at[w, stages, block], recv_w.at[w, block], ctx=(row + 1) % c,
-        )
-
-    def forward(w, s, block, mine):
-        if s != relay:
-            weight_copy(w, s, block, mine).start()
-            return
-
-        @pl.when((block // (2 * (n >> (s + 1)))) % 2 == row)
-        def _():
-            weight_copy(w, s, block, mine).start()
-
     others(lambda to: cond_copy(to, me).start())
     for w in range(4):
         for s in range(stages):
-            forward(w, s, me, True)
+            weight_copy(w, s, me, True).start()
     others(lambda to: small_copy(to, me).start())
     siblings(lambda to: tok_copy(to, row).start())
     for w in range(4):
@@ -173,20 +156,14 @@
         mask = n >> (s + 1)
         origin = flip(me, mask) % (2 * mask)
 
-        def arrived(t, s=s, mask=mask, origin=origin, across=False):
+        def arrived(t, s=s, mask=mask, origin=origin):
             block = origin + t * (2 * mask)
             for w in range(4):
                 weight_copy(w, s, block, False).wait_recv()
-                if across:
-                    relay_copy(w, block).start()
                 for later in range(s + 1, stages):
-                    forward(w, later, block, False)
-
-        if s == relay:
-            loop(1 << (s - 1), lambda t: arrived(2 * t + row, across=True))
-            loop(1 << (s - 1), lambda t: arrived(2 * t + 1 - row))
-        else:
-            loop(1 << s, arrived)
+                    weight_copy(w, later, block, False).start()
+
+        loop(1 << s, arrived)
 
     others(lambda peer: mod_copy(peer, peer).wait_recv())
     total = mod_all[0]
@@ -203,16 +180,7 @@
             for w in range(4):
                 weight_copy(w, s, block, False).wait_send()
 
-        def crossed(t, mask=mask):
-            block = flip(me, mask) % (2 * mask) + t * (2 * mask)
-            for w in range(4):
-                relay_copy(w, block).wait_send()
-
-        if s == relay:
-            loop(1 << (s - 1), lambda t: left(2 * t + row))
-            loop(1 << (s - 1), lambda t: crossed(2 * t + row))
-        else:
-            loop(1 << s, left)
+        loop(1 << s, left)
     others(lambda to: cond_copy(to, me).wait_send())
     others(lambda to: small_copy(to, me).wait_send())
     others(lambda to: mod_copy(to, me).wait_send())
@@ -242,7 +210,7 @@
             pltpu.VMEM(cond.shape, F32),
             pltpu.VMEM((n, *ada_bias.shape), F32),
             pltpu.VMEM((n, *ada_bias.shape), F32),
-            dma((4, stages + 1, n)), dma((4, n)),
+            dma((4, stages, n)), dma((4, n)),
             dma((c,)), dma((c,)), dma((n,)), dma((n,)), dma((n,)), dma((n,)), dma((n,)), dma((n,)),
         ],
         compiler_params=pltpu.CompilerParams(collective_id=0, has_side_effects=True),

time: 143 us -> 140 us (0.979)
  Pallas kernels: 119 us -> 115 us
    pallas_call x1, Pallas kernels: 48.5 us -> 43.3 us  [gather(): pl.pallas_call(partial(gather_kernel, n, c), out_shape=[shape((n, *w.shap...]
    pallas_call x1, Pallas kernels: 56.2 us -> 57.7 us  [reduce(): pl.pallas_call(partial(reduce_kernel, n, c), out_shape=[shape(w.shape[1:]...]
where the time goes in v3:
time: 140 us; the launch traced here: 139 us
  Pallas kernels  115 us (82%)
  local copies, waits for them, and re-layouts  17.3 us (12%)
  other arithmetic  5.82 us (4%)
    pallas_call x1, Pallas kernels, reduce(): pl.pallas_call(partial(reduce_kernel, n, c), out_shape=[shape(w.shape[1:]...  57.7 us
    pallas_call x1, Pallas kernels, gather(): pl.pallas_call(partial(gather_kernel, n, c), out_shape=[shape((n, *w.shap...  43.3 us
    pallas_call x1, Pallas kernels, block(): pl.pallas_call(partial(block_kernel, c), out_shape=[shape(cot.shape, BF16...  14.1 us
    unnamed x20, local copies, waits for them, and re-layouts  6.78 us
    squeeze x3, local copies, waits for them, and re-layouts, per_device(): lax.dynamic_slice(total_line, (0, start + me * size), (1, size))[0]  3.82 us

profile of v3, /device:TPU:0, one launch (start us, length us, event | category | flops | bytes accessed | tf_op | source)
XLA Modules:
  0.0 139.1 jit_solution(6638292147714470705)
XLA Ops:
  0.7 0.7 broadcast_in_dim.41
  1.5 0.7 convert_reduce_fusion
  2.3 0.8 broadcast_in_dim.32.cond
  3.1 1.3 fusion.9
  4.5 43.3 %gather.1 = (bf16[16,24,1152]{2,1,0:T(8,128)(2,1)}, bf16[16,24,384]{2,1,0:T(8,128)(2,1)}, bf16[16,24,1536]{2,1,0:T(8,128)(2,1)}, bf16[16,96,384]{2,1,0:T(8,128)(...) custom-call(bf16[24,1152]{1,0:T(8,128)(2,1)} %qkv.1, ...), custom_call_target="tpu_custom_call" | custom-call | tf_op jit(solution)/shard_map/gather/pallas_call | solution.py:198
  47.8 0.8 slice_reduce_fusion.3
  48.8 0.8 slice_reduce_fusion.2
  49.7 0.7 slice_reduce_fusion.4
  51.1 0.9 dynamic-slice_bitcast_fusion
  52.1 0.8 pad_maximum_fusion.tok_ref
  52.9 14.1 %block.1 = (bf16[256,384]{1,0:T(8,128)(2,1)}, f32[256,384]{1,0:T(8,128)}, f32[256,384]{1,0:T(8,128)}, bf16[1,256,384]{2,1,0:T(8,128)(2,1)}, bf16[384,1152]{1,0:T...) custom-call(bf16[384,1152]{1,0:T(8,128)(2,1)} %bitcast.32, ...), custom_call_target="tpu_custom_call" | custom-call | tf_op jit(solution)/shard_map/block/pallas_call | solution.py:537
  67.0 1.1 pad_convert_fusion.ada
  68.1 57.7 %reduce.23 = (f32[24,1152]{1,0:T(8,128)}, f32[24,384]{1,0:T(8,128)}, f32[24,1536]{1,0:T(8,128)}, f32[96,384]{1,0:T(8,128)}, bf16[256,384]{1,0:T(8,128)(2,1)}, /*...) custom-call(bf16[16,24,1152]{2,1,0:T(8,128)(2,1)} %bitcast.33, bf16[16,24,384]{2,1,0:T(8,128)(2,1)} %bitcast.35, ...), custom_call_target="tpu_custom_call" | custom-call | tf_op jit(solution)/shard_map/reduce/pallas_call | solution.py:401
  125.9 1.3 fusion.13
  127.2 0.7 slice_reduce_fusion
  128.6 1.2 fusion.10
  129.8 1.3 fusion.12
  131.1 1.3 constant_dynamic-slice_fusion.4
  132.4 1.6 %copy.33 = bf16[1,256,384]{2,1,0:T(8,128)(2,1)} copy(bf16[1,256,384]{2,1,0:T(8,128)(2,1)} %bitcast.36) | data formatting | bytes 393216
  134.0 1.6 %copy.34 = f32[24,2304]{1,0:T(8,128)} copy(f32[24,2304]{1,0:T(8,128)} %get-tuple-element.85) | data formatting | bytes 442368
  135.6 1.5 %copy.35 = f32[24,1152]{1,0:T(8,128)} copy(f32[24,1152]{1,0:T(8,128)} %get-tuple-element.87) | data formatting | bytes 221184
  137.2 0.6 copy.36
  137.8 0.7 copy.37
  138.5 0.7 copy.38
  (24 shorter events, 1.9 us)
Async XLA Ops:
  0.6 51.4 %copy-start = (bf16[1,256,384]{2,1,0:T(8,128)(2,1)S(1)}, bf16[1,256,384]{2,1,0:T(8,128)(2,1)}, u32[]{:S(2)}) copy-start(bf16[1,256,384]{2,1,0:T(8,128)(2,1)} %param.13) | copy-start | bytes 589828
  1.5 3.0 %copy-start.5 = (f32[1,2304]{1,0:T(1,128)}, f32[1,2304]{1,0:T(1,128)S(1)}, u32[]{:S(2)}) copy-start(f32[1,2304]{1,0:T(1,128)S(1)} %dynamic_update_slice.3.ada_bias) | copy-start | bytes 27652
  52.9 14.1 %copy-start.1 = (bf16[24,2304]{1,0:T(8,128)(2,1)S(1)}, bf16[24,2304]{1,0:T(8,128)(2,1)}, u32[]{:S(2)}) copy-start(bf16[24,2304]{1,0:T(8,128)(2,1)} %ada.1) | copy-start | bytes 331780
  68.1 59.9 %copy-start.6 = (bf16[1,384]{1,0:T(2,128)(2,1)S(1)}, bf16[1,384]{1,0:T(2,128)(2,1)}, u32[]{:S(2)}) copy-start(bf16[1,384]{1,0:T(2,128)(2,1)} %param.14) | copy-start | bytes 2308
  125.8 11.3 %copy-start.4 = (f32[24,384]{1,0:T(8,128)S(1)}, f32[24,384]{1,0:T(8,128)}, u32[]{:S(2)}) copy-start(f32[24,384]{1,0:T(8,128)} %get-tuple-element.89) | copy-start | bytes 110596
  125.9 11.9 %copy-start.3 = (f32[24,1536]{1,0:T(8,128)S(1)}, f32[24,1536]{1,0:T(8,128)}, u32[]{:S(2)}) copy-start(f32[24,1536]{1,0:T(8,128)} %get-tuple-element.91) | copy-start | bytes 442372
  125.9 12.6 %copy-start.2 = (f32[96,384]{1,0:T(8,128)S(1)}, f32[96,384]{1,0:T(8,128)}, u32[]{:S(2)}) copy-start(f32[96,384]{1,0:T(8,128)} %get-tuple-element.93) | copy-start | bytes 442372
